TPU v7x, 128 devices: a whole 4x4x4 slice. The times are simulated.
128 devices in a mesh: inner: 32 (over z_lo, x, y), outer: 4 (over z_hi, core).
Axes of the slice: x: 4, y: 4, z: 4 (z_hi: 2, z_lo: 2; z = z_hi * 2 + z_lo), core: 2. Of those that a mesh axis runs over, the one named last changes fastest.
Arguments:
- hidden: bfloat16 [32768, 1152], P(('inner', 'outer')), may hold values from -6 to 6
- latents_now: float32 [128, 16, 256], P(('inner', 'outer')), may hold values from -6 to 6
- latents_next: float32 [128, 16, 256], P(('inner', 'outer')), may hold values from -6.3 to 6.3
- timestep: int32 [1], replicated, may hold values from 3 to 9
- version_tags: int32 [128], P(('inner', 'outer')), may hold values from 0 to 7
- noise_levels: float32 [8], replicated, may hold values from 0.5 to 1
- time_weight: bfloat16 [256, 6912], replicated, may hold values from -0.375 to 0.375
- spatial_qkv: bfloat16 [1152, 3456], replicated, may hold values from -0.1875 to 0.1875
- spatial_out: bfloat16 [1152, 1152], replicated, may hold values from -0.1875 to 0.1875
- temporal_qkv: bfloat16 [1152, 3456], replicated, may hold values from -0.1875 to 0.1875
- temporal_out: bfloat16 [1152, 1152], replicated, may hold values from -0.1875 to 0.1875
- final_weight: bfloat16 [16, 1152], replicated, may hold values from -0.1875 to 0.1875
Outputs:
- log_prob: float32 [128, 256], P(('inner', 'outer'))
- next_mean: float32 [128, 16, 256], P(('inner', 'outer'))
Inputs may be any that keep to these rules, and one draw needn't show every extreme that they name: `timestep`: the index k of the denoising step, whose time is k / 10.
All inputs are finite; a program needn't handle non-finite values.
Results may differ from a plain program's by a relative error of at most 0.004.
Values may be sent and summed in bfloat16 or wider, within the bound.
No kernel may reach another device: no remote copies, remote signals or barrier semaphores. Data moves between devices by JAX's collectives and lax.ppermute only.
A program may use at most 128 MiB of HBM per device.

v0:
```python
import math

import jax
import jax.numpy as jnp
from jax import lax
from jax.sharding import PartitionSpec as P

D = 1152
HEADS = 16
FREQ = 256
STEPS = 10
VERSIONS = 8


norm_eps = 1e-06


def layer_norm(values):
    average = jnp.mean(values, -1, keepdims=True)
    centred = values - average
    variance = jnp.mean(centred * centred, -1, keepdims=True)
    return centred * lax.rsqrt(variance + norm_eps)


def head_norm(values):
    return values * lax.rsqrt(jnp.mean(values * values, -1, keepdims=True) + norm_eps)


def modulation(timestep, time_weight):
    half_width = FREQ // 2
    time_value = timestep.astype(jnp.float32) / STEPS
    frequencies = jnp.exp(
        -math.log(10000.0) * jnp.arange(half_width).astype(jnp.float32) / half_width
    )
    angles = 1000.0 * time_value[:, None] * frequencies[None, :]
    embedded = jnp.concatenate([jnp.cos(angles), jnp.sin(angles)], 1)
    activated = jax.nn.silu(embedded).astype(jnp.bfloat16)
    return jnp.dot(activated, time_weight, preferred_element_type=jnp.float32)[0]


def project_rows(normed, qkv_weight):
    rows = normed.shape[0]
    head_width = D // HEADS
    mixed = jnp.dot(normed, qkv_weight, preferred_element_type=jnp.float32)
    queries = head_norm(mixed[:, :D].reshape(rows, HEADS, head_width)) * head_width ** (-0.5)
    key_rows = head_norm(mixed[:, D : 2 * D].reshape(rows, HEADS, head_width))
    return jnp.concatenate(
        [queries.reshape(rows, D), key_rows.reshape(rows, D), mixed[:, 2 * D :]], 1
    ).astype(jnp.bfloat16)


def spatial_block(hidden, shift_s, scale_s, gate_s, spatial_qkv, spatial_out):
    tokens = hidden.shape[0]
    head_width = D // HEADS
    normed = (layer_norm(hidden.astype(jnp.float32)) * (1.0 + scale_s) + shift_s).astype(
        jnp.bfloat16
    )
    packed = project_rows(normed, spatial_qkv)
    key_rows = packed[:, D : 2 * D].reshape(tokens, HEADS, head_width)
    value_rows = packed[:, 2 * D :].reshape(tokens, HEADS, head_width)
    block_rows = min(tokens, 512)
    query_blocks = packed[:, :D].reshape(tokens // block_rows, block_rows, HEADS, head_width)

    def one_block(query_rows):
        scores = jnp.einsum(
            "qhe,khe->hqk", query_rows, key_rows, preferred_element_type=jnp.float32
        )
        weights = jnp.exp(scores)
        weights = (weights / jnp.sum(weights, -1, keepdims=True)).astype(jnp.bfloat16)
        mixed = jnp.einsum("hqk,khe->qhe", weights, value_rows, preferred_element_type=jnp.float32)
        return mixed.astype(jnp.bfloat16).reshape(block_rows, D)

    attended = lax.map(one_block, query_blocks).reshape(tokens, D)
    projected = jnp.dot(attended, spatial_out, preferred_element_type=jnp.float32)
    return (hidden.astype(jnp.float32) + gate_s * projected).astype(jnp.bfloat16)


def shards(
    hidden,
    latents_now,
    latents_next,
    timestep,
    version_tags,
    noise_levels,
    time_weight,
    spatial_qkv,
    spatial_out,
    temporal_qkv,
    temporal_out,
    final_weight,
):
    table = modulation(timestep, time_weight)
    shift_s = table[0:D]
    scale_s = table[D : 2 * D]
    gate_s = table[2 * D : 3 * D]
    shift_t = table[3 * D : 4 * D]
    scale_t = table[4 * D : 5 * D]
    gate_t = table[5 * D : 6 * D]
    head_width = D // HEADS
    tokens = hidden.shape[0]
    after_spatial = spatial_block(hidden, shift_s, scale_s, gate_s, spatial_qkv, spatial_out)
    normed = (layer_norm(after_spatial.astype(jnp.float32)) * (1.0 + scale_t) + shift_t).astype(
        jnp.bfloat16
    )
    outgoing = project_rows(normed, temporal_qkv)
    peers = lax.axis_size(("inner", "outer"))
    blocks = outgoing.reshape(peers, 1, tokens // peers, outgoing.shape[1])
    arrived = lax.all_to_all(blocks, ("inner", "outer"), split_axis=0, concat_axis=1, tiled=True)
    frames = arrived.shape[1]
    count = arrived.shape[2]
    width = arrived.shape[3]
    flat_rows = arrived.reshape(frames, count, width)
    query_rows = flat_rows[:, :, :D].reshape(frames, count, HEADS, head_width)
    key_rows = flat_rows[:, :, D : 2 * D].reshape(frames, count, HEADS, head_width)
    value_rows = flat_rows[:, :, 2 * D :].reshape(frames, count, HEADS, head_width)
    scores = jnp.einsum("fnhe,gnhe->nhfg", query_rows, key_rows, preferred_element_type=jnp.float32)
    weights = jnp.exp(scores)
    weights = (weights / jnp.sum(weights, -1, keepdims=True)).astype(jnp.bfloat16)
    mixed = jnp.einsum("nhfg,gnhe->fnhe", weights, value_rows, preferred_element_type=jnp.float32)
    mixed = mixed.astype(jnp.bfloat16).reshape(frames * count, D)
    projected = jnp.dot(mixed, temporal_out, preferred_element_type=jnp.float32).astype(
        jnp.bfloat16
    )
    worked = projected.reshape(1, frames, count, D)
    returned = lax.all_to_all(worked, ("inner", "outer"), split_axis=1, concat_axis=0, tiled=True)
    temporal_term = returned.reshape(tokens, D)
    final_state = after_spatial.astype(jnp.float32) + gate_t * temporal_term.astype(jnp.float32)
    final_normed = layer_norm(final_state).astype(jnp.bfloat16)
    velocity = jnp.einsum(
        "cd,td->ct", final_weight, final_normed, preferred_element_type=jnp.float32
    )[None]
    time_value = timestep.astype(jnp.float32)[0] / STEPS
    matches = (version_tags[:, None] == jnp.arange(VERSIONS)[None, :]).astype(jnp.float32)
    levels = jnp.sum(noise_levels[None, :] * matches, 1)
    noise_scale = levels * jnp.sqrt(time_value / (1.0 - time_value))
    factor = (noise_scale * noise_scale / (2.0 * time_value))[:, None, None]
    drift = velocity + factor * (latents_now + (1.0 - time_value) * velocity)
    next_mean = latents_now - drift / STEPS
    spread = noise_scale * math.sqrt(1.0 / STEPS)
    standard = (latents_next - next_mean) / spread[:, None, None]
    log_prob = (
        -0.5 * jnp.mean(standard * standard, 1)
        - jnp.log(spread)[:, None]
        - 0.5 * math.log(2.0 * math.pi)
    )
    return (log_prob, next_mean)


def solution(mesh):
    return jax.shard_map(
        shards,
        mesh=mesh,
        in_specs=(
            P(("inner", "outer"), None),
            P(("inner", "outer"), None, None),
            P(("inner", "outer"), None, None),
            P(),
            P(("inner", "outer")),
            P(),
            P(),
            P(),
            P(),
            P(),
            P(),
            P(),
        ),
        out_specs=(P(("inner", "outer"), None), P(("inner", "outer"), None, None)),
        check_vma=False,
    )
```

profile of v0, /device:TPU:1, one launch (start us, length us, event | category | flops | bytes accessed | tf_op | source)
XLA Modules:
  0.0 144.2 jit_solution(15985870924821026586)
XLA Ops:
  4.4 6.0 %fusion.14 = f32[256,3456]{1,0:T(8,128)S(1)} fusion(bf16[1152,3456]{1,0:T(8,128)(2,1)} %param.19, bf16[256,1152]{1,0:T(8,128)(2,1)S(1)} %copy-done.7, f32[1152]{0:T(1024)S(1)} %get-tuple-element.33, f32[1152]{0:T(1024)S(1)} %get-tuple-element.34, f32[256]{0:T(256)S(1)} %add_rsqrt_fusion.6, f32[256]{0:T(256)S(1)} %broadcast_multiply_fusion.2), kind=kOutput, calls=%fused_computation.40 | convolution fusion | flops 2040201216 | bytes 12102656 | tf_op jit(solution)/shard_map/dot_general | solution.py:44
  11.2 1.6 %slice_multiply_fusion.2 = (f32[256,1152]{1,0:T(8,128)}, f32[256,1152]{1,0:T(8,128)}) fusion(f32[256,3456]{1,0:T(8,128)S(1)} %fusion.14), kind=kLoop, calls=%fused_computation.36 | loop fusion | flops 589824 | bytes 4718592 | tf_op jit(solution)/shard_map/mul | solution.py:26
  12.8 2.1 %copy.39 = bf16[256,1152]{0,1:T(8,128)(2,1)} copy(bf16[256,1152]{1,0:T(8,128)(2,1)} %slice.102) | data formatting | bytes 1179648 | tf_op jit(solution)/shard_map/slice | solution.py:48
  14.9 2.7 %copy.43 = f32[256,1152]{0,1:T(8,128)} copy(f32[256,1152]{1,0:T(8,128)} %get-tuple-element.25) | data formatting | bytes 2359296 | tf_op jit(solution)/shard_map/mul | solution.py:26
  20.1 2.7 %copy.44 = f32[256,1152]{1,0:T(8,128)} copy(f32[256,1152]{0,1:T(8,128)} %bitcast.70) | data formatting | bytes 2359296 | tf_op jit(solution)/shard_map/mul | solution.py:26
  22.8 2.7 %copy.40 = f32[256,1152]{0,1:T(8,128)} copy(f32[256,1152]{1,0:T(8,128)} %get-tuple-element.26) | data formatting | bytes 2359296 | tf_op jit(solution)/shard_map/mul | solution.py:26
  27.9 2.6 %copy.41 = f32[256,1152]{1,0:T(8,128)} copy(f32[256,1152]{0,1:T(8,128)} %bitcast.72) | data formatting | bytes 2359296 | tf_op jit(solution)/shard_map/mul | solution.py:26
  30.6 2.9 %multiply_convert_fusion.3 = (bf16[256,1152]{1,0:T(8,128)(2,1)}, bf16[256,1152]{1,0:T(8,128)(2,1)}) fusion(f32[256,1152]{1,0:T(8,128)} %copy.44, f32[256,3456]{1,0:T(8,128)S(1)} %fusion.14, f32[256,1152]{1,0:T(8,128)} %copy.41), kind=kLoop, calls=%fused_computation.31 | loop fusion | flops 1474560 | bytes 5898240 | tf_op jit(solution)/shard_map/slice | solution.py:59
  40.4 2.7 %fusion.12 = f32[256,3456]{1,0:T(8,128)S(1)} fusion(bf16[1152,3456]{1,0:T(8,128)(2,1)S(1)} %bitcast.87, f32[256,1152]{1,0:T(8,128)S(1)} %get-tuple-element.39, f32[1152]{0:T(1024)S(1)} %copy-done.15, f32[1152]{0:T(1024)S(1)} %copy-done.16, f32[256]{0:T(256)S(1)} %add_rsqrt_fusion.5, f32[256]{0:T(256)S(1)} %broadcast_multiply_fusion.1), kind=kOutput, calls=%fused_computation.38 | convolution fusion | flops 2039906304 | bytes 12692480 | tf_op jit(solution)/shard_map/dot_general | solution.py:44
  44.0 1.6 %slice_multiply_fusion.1 = (f32[256,1152]{1,0:T(8,128)}, f32[256,1152]{1,0:T(8,128)}) fusion(f32[256,3456]{1,0:T(8,128)S(1)} %fusion.12), kind=kLoop, calls=%fused_computation.35 | loop fusion | flops 589824 | bytes 4718592 | tf_op jit(solution)/shard_map/mul | solution.py:26
  45.6 2.6 %concatenate.31 = bf16[128,1,2,1152]{3,2,0,1:T(2,128)(2,1)} reshape(bf16[256,1152]{1,0:T(8,128)(2,1)} %slice.101) | data formatting | bytes 1179648 | tf_op jit(solution)/shard_map/concatenate | solution.py:47
  48.2 2.6 %copy.47 = f32[256,1152]{0,1:T(8,128)} copy(f32[256,1152]{1,0:T(8,128)} %get-tuple-element.21) | data formatting | bytes 2359296 | tf_op jit(solution)/shard_map/mul | solution.py:26
  50.9 1.4 reduce_sum.134
  53.3 2.7 %copy.48 = f32[256,1152]{1,0:T(8,128)} copy(f32[256,1152]{0,1:T(8,128)} %bitcast.74) | data formatting | bytes 2359296 | tf_op jit(solution)/shard_map/mul | solution.py:26
  56.0 2.6 %copy.49 = f32[256,1152]{0,1:T(8,128)} copy(f32[256,1152]{1,0:T(8,128)} %get-tuple-element.22) | data formatting | bytes 2359296 | tf_op jit(solution)/shard_map/mul | solution.py:26
  61.1 2.7 %copy.50 = f32[256,1152]{1,0:T(8,128)} copy(f32[256,1152]{0,1:T(8,128)} %bitcast.75) | data formatting | bytes 2359296 | tf_op jit(solution)/shard_map/mul | solution.py:26
  63.8 2.9 %multiply_convert_fusion.2 = (bf16[256,1152]{1,0:T(8,128)(2,1)}, bf16[256,1152]{1,0:T(8,128)(2,1)}) fusion(f32[256,1152]{1,0:T(8,128)} %copy.48, f32[256,3456]{1,0:T(8,128)S(1)} %fusion.12, f32[256,1152]{1,0:T(8,128)} %copy.50), kind=kLoop, calls=%fused_computation.28 | loop fusion | flops 1474560 | bytes 5898240 | tf_op jit(solution)/shard_map/convert.7
  66.6 2.0 %concatenate.30 = bf16[128,1,2,1152]{3,2,0,1:T(2,128)(2,1)S(1)} reshape(bf16[256,1152]{1,0:T(8,128)(2,1)} %get-tuple-element.20) | data formatting | bytes 1179648 | tf_op jit(solution)/shard_map/concatenate | solution.py:47
  69.7 3.0 %pad_maximum_fusion = bf16[128,1,2,3456]{3,2,1,0:T(2,128)(2,1)S(1)} fusion(bf16[128,1,2,1152]{3,2,1,0:T(2,128)(2,1)S(1)} %bitcast.76, bf16[128,1,2,1152]{3,2,1,0:T(2,128)(2,1)S(1)} %bitcast.78, bf16[128,1,2,1152]{3,2,1,0:T(2,128)(2,1)} %bitcast.80), kind=kLoop, calls=%fused_computation.10 | loop fusion | flops 5308416 | bytes 3538944 | tf_op jit(solution)/shard_map/concatenate | solution.py:47
  72.7 38.0 %all_to_all.8 = bf16[128,1,2,3456]{3,2,1,0:T(2,128)(2,1)S(1)} all-to-all(bf16[128,1,2,3456]{3,2,1,0:T(2,128)(2,1)S(1)} %pad_maximum_fusion), channel_id=1, replica_groups=mesh['inner'=32,'outer'=4] {'inner','outer'}, dimensions={0} | all-to-all | bytes 3538944 | tf_op jit(solution)/shard_map/all_to_all | solution.py:108
  111.9 1.8 %copy.54 = bf16[128,2,1152]{0,2,1:T(8,128)(2,1)} copy(bf16[128,2,1152]{2,1,0:T(2,128)(2,1)S(1)} %get-tuple-element.29) | data formatting | bytes 1179648 | tf_op jit(solution)/shard_map/slice | solution.py:115
  118.9 2.8 %convolution_convert_fusion = bf16[256,1152]{1,0:T(8,128)(2,1)S(1)} fusion(bf16[256,1152]{1,0:T(8,128)(2,1)S(1)} %reshape.282, bf16[1152,1152]{1,0:T(8,128)(2,1)} %param.22), kind=kOutput, calls=%fused_computation.4 | convolution fusion | flops 679772160 | bytes 3833856 | tf_op jit(solution)/shard_map/dot_general | solution.py:121
  122.7 4.6 %all-to-all-start.1 = ((bf16[1,128,2,1152]{3,2,0,1:T(2,128)(2,1)}), bf16[1,128,2,1152]{3,2,0,1:T(2,128)(2,1)S(1)}, u32[]{:S(2)}, u32[]{:S(2)}) async-start(bf16[1,128,2,1152]{3,2,0,1:T(2,128)(2,1)} %bitcast.22), calls=%async_computation.1 | async-start | bytes 1179648 | tf_op jit(solution)/shard_map/all_to_all | solution.py:125
  129.6 11.9 %all-to-all-done.1 = bf16[1,128,2,1152]{3,2,0,1:T(2,128)(2,1)S(1)} async-done(((bf16[1,128,2,1152]{3,2,0,1:T(2,128)(2,1)}), bf16[1,128,2,1152]{3,2,0,1:T(2,128)(2,1)S(1)}, u32[]{:S(2)}, u32[]{:S(2)}) %all-to-all-start.1) | async-done | bytes 589856 | tf_op jit(solution)/shard_map/all_to_all | solution.py:125
  (92 shorter events, 31.9 us)
Async XLA Ops:
  0.6 2.0 %copy-start = (bf16[256,6912]{1,0:T(8,128)(2,1)S(1)}, bf16[256,6912]{1,0:T(8,128)(2,1)}, u32[]{:S(2)}) copy-start(bf16[256,6912]{1,0:T(8,128)(2,1)} %param.18) | copy-start | bytes 10616836
  2.7 1.2 copy-start.7
  33.4 1.4 copy-start.4
  35.1 1.1 copy-start.9
  35.1 4.9 %slice-start = ((s8[7962624]{0:T(1024)(128)(4,1)}), s8[4194304]{0:T(1024)(128)(4,1)S(1)}, s32[]{:S(2)}) async-start(s8[7962624]{0:T(1024)(128)(4,1)} %bitcast.86), calls=%async_computation.2 | async-start | bytes 8388608
  36.1 1.4 copy-start.8
  36.1 1.4 copy-start.17
  36.1 2.3 %copy-start.18 = (bf16[1152,1152]{1,0:T(8,128)(2,1)S(1)}, bf16[1152,1152]{1,0:T(8,128)(2,1)}, u32[]{:S(2)}) copy-start(bf16[1152,1152]{1,0:T(8,128)(2,1)} %param.20) | copy-start | bytes 7962628
  36.1 3.8 %slice-start.1 = ((s8[7962624]{0:T(1024)(128)(4,1)}), s8[3768320]{0:T(1024)(128)(4,1)S(1)}, s32[]{:S(2)}) async-start(s8[7962624]{0:T(1024)(128)(4,1)} %bitcast.86), calls=%async_computation.3 | async-start | bytes 7536640
  39.6 3.6 %copy-start.2 = (f32[256,1152]{1,0:T(8,128)}, f32[256,1152]{1,0:T(8,128)S(1)}, u32[]{:S(2)}) copy-start(f32[256,1152]{1,0:T(8,128)S(1)} %get-tuple-element.39) | copy-start | bytes 3538948
  39.6 0.7 copy-start.15
  39.6 0.8 copy-start.16
  66.6 2.0 %copy-start.5 = (bf16[256,1152]{1,0:T(8,128)(2,1)S(1)}, bf16[256,1152]{1,0:T(8,128)(2,1)}, u32[]{:S(2)}) copy-start(bf16[256,1152]{1,0:T(8,128)(2,1)} %get-tuple-element.14) | copy-start | bytes 1769476
  66.6 3.1 %copy-start.6 = (bf16[128,1,2,1152]{3,2,0,1:T(2,128)(2,1)S(1)}, bf16[128,1,2,1152]{3,2,0,1:T(2,128)(2,1)}, u32[]{:S(2)}) copy-start(bf16[128,1,2,1152]{3,2,0,1:T(2,128)(2,1)} %concatenate.31) | copy-start | bytes 1769476
  115.1 1.1 copy-start.10
  121.7 6.6 %copy-start.19 = (f32[8]{0:T(128)S(1)}, f32[8]{0:T(128)}, u32[]{:S(2)}) copy-start(f32[8]{0:T(128)} %param.17) | copy-start | bytes 100
  122.7 18.7 %all-to-all-start.1 = ((bf16[1,128,2,1152]{3,2,0,1:T(2,128)(2,1)}), bf16[1,128,2,1152]{3,2,0,1:T(2,128)(2,1)S(1)}, u32[]{:S(2)}, u32[]{:S(2)}) async-start(bf16[1,128,2,1152]{3,2,0,1:T(2,128)(2,1)} %bitcast.22), calls=%async_computation.1 | async-start | bytes 1179648 | tf_op jit(solution)/shard_map/all_to_all | solution.py:125
  127.4 14.3 %copy-start.3 = (f32[256,1152]{1,0:T(8,128)S(1)}, f32[256,1152]{1,0:T(8,128)}, u32[]{:S(2)}) copy-start(f32[256,1152]{1,0:T(8,128)} %copy-done.2) | copy-start | bytes 3538948
  127.4 14.3 %copy-start.12 = (f32[1152]{0:T(1024)S(1)}, f32[1152]{0:T(1024)}, u32[]{:S(2)}) copy-start(f32[1152]{0:T(1024)} %get-tuple-element.30) | copy-start | bytes 13828
  141.9 0.8 copy-start.11
  141.9 0.8 copy-start.13
  141.9 0.8 copy-start.14
  141.9 2.3 %copy-start.1 = (bf16[256,6912]{1,0:T(8,128)(2,1)S(1)}, bf16[256,6912]{1,0:T(8,128)(2,1)}, u32[]{:S(2)}) copy-start(bf16[256,6912]{1,0:T(8,128)(2,1)} %param.18) | copy-start | bytes 10616836
where the time goes:
time: 145 us; the launch traced here: 144 us
  local copies, waits for them, and re-layouts  48.9 us (34%)
  blocking collectives  38 us (26%)
  other arithmetic  20.4 us (14%)
  matrix products  16.9 us (12%)
  waiting for transfers between devices  11.9 us (8%)
  starting transfers between devices  4.63 us (3%)
  between operations  3.4 us (2%)
    all_to_all x1, blocking collectives, shards(): lax.all_to_all(blocks, ('inner', 'outer'), split_axis=0, concat_axis=1, t...  38 us
    mul x8, local copies, waits for them, and re-layouts, head_norm(): values * lax.rsqrt(jnp.mean(values * values, -1, keepdims=True) + norm_eps)  15 us
    all_to_all x1, waiting for transfers between devices, shards(): lax.all_to_all(worked, ('inner', 'outer'), split_axis=1, concat_axis=0, t...  11.9 us
    mul x4, local copies, waits for them, and re-layouts, head_norm(): values * values  10.6 us
    dot_general x2, matrix products, project_rows(): mixed = jnp.dot(normed, qkv_weight, preferred_element_type=jnp.float32)  8.73 us
    concatenate x3, local copies, waits for them, and re-layouts, project_rows(): jnp.concatenate([queries.reshape(rows, D), key_rows.reshape(rows, D), mix...  5.67 us
    reduce_sum x4, other arithmetic, head_norm(): jnp.mean(values * values, -1, keepdims=True) + norm_eps  5.47 us
    all_to_all x1, starting transfers between devices, shards(): lax.all_to_all(worked, ('inner', 'outer'), split_axis=1, concat_axis=0, t...  4.63 us
  transfers between devices with their start and end apart: 1, of which 1 were waited for; matrix products, arithmetic and copies ran while one was open for 0% of the time, Pallas kernels for 0%

commit v1 on v0

v1 whole, which is shorter than its diff:
```python
import math

import jax
import jax.numpy as jnp
from jax import lax
from jax.experimental import pallas as pl
from jax.experimental.pallas import tpu as pltpu
from jax.sharding import PartitionSpec as P

D = 1152
HEADS = 16
HEAD = D // HEADS
C = 16
FREQ = 256
STEPS = 10
VERSIONS = 8
TPF = 256
LANES = 128
CHUNKS = tuple((low, min(512, 3 * D - low)) for low in range(0, 3 * D, 512))
ROWS = 32

norm_eps = 1e-06
f32 = jnp.float32
bf16 = jnp.bfloat16


def iota(shape, dim):
    return lax.broadcasted_iota(jnp.int32, shape, dim)


def centre(values):
    centred = values - jnp.mean(values, -1, keepdims=True)
    variance = jnp.mean(centred * centred, -1, keepdims=True)
    return centred * lax.rsqrt(variance + norm_eps)


def fill_picker(picker):
    for low in range(0, 2 * D, 256):
        column = iota((256, LANES), 0) + low
        lane = iota((256, LANES), 1)
        head = jnp.where(lane < 2 * HEADS, lane, lane - 2 * HEADS)
        offset = column - head * HEAD
        inside = (offset >= 0) & (offset < HEAD) & (lane < 4 * HEADS)
        picker[low : low + 256, :] = jnp.where(inside, 1.0, 0.0).astype(bf16)


def modulate_rows(source, scale, shift, normed):
    def step(index, carry):
        rows = pl.ds(pl.multiple_of(index * ROWS, ROWS), ROWS)
        values = centre(source[rows, :].astype(f32))
        normed[rows, :] = (values * (1.0 + scale) + shift).astype(bf16)
        return carry

    lax.fori_loop(0, TPF // ROWS, step, 0)


def project(normed, weight, picker, raw, packed, ready):
    squares = jnp.zeros((TPF, LANES), f32)
    for index, (low, width) in enumerate(CHUNKS):
        ready(index)
        mixed = jnp.dot(normed[...], weight[:, low : low + width], preferred_element_type=f32)
        part = min(max(2 * D - low, 0), width)
        if part:
            wanted = mixed[:, :part]
            raw[:, low : low + part] = wanted
            squares = squares + jnp.dot(
                (wanted * wanted).astype(bf16),
                picker[low : low + part, :],
                preferred_element_type=f32,
            )
        if part < width:
            packed[:, low + part : low + width] = mixed[:, part:].astype(bf16)
    lane = iota((TPF, LANES), 1)
    head = jnp.where(lane < 2 * HEADS, lane, lane - 2 * HEADS)
    factor = lax.rsqrt(squares * (1.0 / HEAD) + norm_eps)
    factor = factor * jnp.where(head < HEADS, HEAD ** (-0.5) * math.log2(math.e), 1.0)
    coarse = factor.astype(bf16)
    fine = (factor - coarse.astype(f32)).astype(bf16)
    both = jnp.where(lane < 2 * HEADS, coarse.astype(f32), fine.astype(f32)).astype(bf16)
    for low in range(0, 2 * D, 256):
        spread = lax.dot_general(
            both,
            picker[low : low + 256, :],
            (((1,), (1,)), ((), ())),
            preferred_element_type=f32,
        )
        packed[:, low : low + 256] = (raw[:, low : low + 256] * spread).astype(bf16)


def attend(packed, attended, same):
    ones = jnp.ones((TPF, LANES), bf16)
    for head in range(HEADS):
        start = head * HEAD
        low = start // LANES * LANES
        high = -(-(start + HEAD) // LANES) * LANES
        width = high - low
        lane = iota((TPF, width), 1) + low
        inside = (lane >= start) & (lane < start + HEAD)
        queries = packed[:, low:high]
        queries = jnp.where(inside, queries, jnp.zeros_like(queries))
        scores = lax.dot_general(
            queries,
            packed[:, D + low : D + high],
            (((1,), (1,)), ((), ())),
            preferred_element_type=f32,
        )
        weights = jnp.exp2(scores).astype(bf16)
        if same is not None:
            weights = weights * same[...]
        total = jnp.dot(weights, ones, preferred_element_type=f32)
        mixed = jnp.dot(weights, packed[:, 2 * D + low : 2 * D + high], preferred_element_type=f32)
        share = 1.0 / total
        for tile in range(low, high, LANES):
            result = mixed[:, tile - low : tile - low + LANES] * share
            if start > tile:
                keep = iota((TPF, LANES), 1) + tile < start
                result = jnp.where(keep, attended[:, tile : tile + LANES].astype(f32), result)
            attended[:, tile : tile + LANES] = result.astype(bf16)


def spatial_kernel(
    step_ref, hidden_hbm, time_hbm, qkv_hbm, out_hbm,
    after_ref, table_ref,
    hidden, time_weight, qkv, out_weight, picker, normed, raw, packed, attended, sems,
):
    copies = [pltpu.make_async_copy(hidden_hbm, hidden, sems.at[0])]
    copies.append(
        pltpu.make_async_copy(
            time_hbm.at[:, 0 : 2 * D], time_weight.at[:, 0 : 2 * D], sems.at[1]
        )
    )
    for index, (low, width) in enumerate(CHUNKS):
        copies.append(
            pltpu.make_async_copy(
                qkv_hbm.at[:, low : low + width], qkv.at[:, low : low + width], sems.at[2 + index]
            )
        )
    last = 2 + len(CHUNKS)
    copies.append(pltpu.make_async_copy(out_hbm, out_weight, sems.at[last]))
    copies.append(
        pltpu.make_async_copy(
            time_hbm.at[:, 2 * D : 6 * D], time_weight.at[:, 2 * D : 6 * D], sems.at[last + 1]
        )
    )
    for copy in copies:
        copy.start()

    fill_picker(picker)
    time_value = jnp.full((16, FREQ // 2), step_ref[0], jnp.int32).astype(f32) / STEPS
    position = iota((16, FREQ // 2), 1).astype(f32)
    angles = 1000.0 * time_value * jnp.exp(-math.log(10000.0) * position / (FREQ // 2))
    embedded = jnp.concatenate([jnp.cos(angles), jnp.sin(angles)], 1)
    activated = (embedded / (1.0 + jnp.exp(-embedded))).astype(bf16)

    copies[0].wait()
    copies[1].wait()
    first = jnp.dot(activated, time_weight[:, 0 : 2 * D], preferred_element_type=f32)
    modulate_rows(hidden, first[0:1, D : 2 * D], first[0:1, 0:D], normed)
    project(normed, qkv, picker, raw, packed, lambda index: copies[2 + index].wait())
    attend(packed, attended, None)
    copies[last].wait()
    copies[last + 1].wait()
    rest = jnp.dot(activated, time_weight[:, 2 * D : 6 * D], preferred_element_type=f32)
    table_ref[...] = rest[0:8, D:]
    gate = rest[0:1, 0:D]
    for low in range(0, D, 256):
        width = min(256, D - low)
        projected = jnp.dot(
            attended[...], out_weight[:, low : low + width], preferred_element_type=f32
        )
        after_ref[:, low : low + width] = (
            hidden[:, low : low + width].astype(f32) + gate[:, low : low + width] * projected
        ).astype(bf16)


def temporal_kernel(
    after_ref, table_ref, qkv, out_weight, final_weight,
    velocity_ref,
    picker, same, normed, raw, packed, attended, term,
):
    fill_picker(picker)
    parity = (iota((TPF, TPF), 0) ^ iota((TPF, TPF), 1)) & 1
    same[...] = jnp.where(parity == 0, 1.0, 0.0).astype(bf16)
    modulate_rows(after_ref, table_ref[0:1, D : 2 * D], table_ref[0:1, 0:D], normed)
    project(normed, qkv, picker, raw, packed, lambda index: None)
    attend(packed, attended, same)
    for low in range(0, D, 256):
        width = min(256, D - low)
        term[:, low : low + width] = jnp.dot(
            attended[...], out_weight[:, low : low + width], preferred_element_type=f32
        ).astype(bf16)
    gate = table_ref[0:1, 2 * D : 3 * D]

    def step(index, carry):
        rows = pl.ds(pl.multiple_of(index * ROWS, ROWS), ROWS)
        state = after_ref[rows, :].astype(f32) + gate * term[rows, :].astype(f32)
        normed[rows, :] = centre(state).astype(bf16)
        return carry

    lax.fori_loop(0, TPF // ROWS, step, 0)
    velocity_ref[:, 0:C] = lax.dot_general(
        normed[...], final_weight[...], (((1,), (1,)), ((), ())), preferred_element_type=f32
    )
    velocity_ref[:, C:] = jnp.zeros((TPF, LANES - C), f32)


def density_kernel(
    step_ref, tag_ref, level_ref, velocity_ref, now_ref, next_ref, log_ref, mean_ref
):
    velocity = velocity_ref[...].T[0:C, :]
    level = jnp.full((1, TPF), level_ref[tag_ref[0]], f32)
    time_value = jnp.full((1, TPF), step_ref[0], jnp.int32).astype(f32) / STEPS
    noise_scale = level * jnp.sqrt(time_value / (1.0 - time_value))
    factor = noise_scale * noise_scale / (2.0 * time_value)
    now = now_ref[0]
    drift = velocity + factor * (now + (1.0 - time_value) * velocity)
    next_mean = now - drift / STEPS
    spread = noise_scale * math.sqrt(1.0 / STEPS)
    standard = (next_ref[0] - next_mean) / spread
    log_ref[...] = (
        -0.5 * jnp.mean(standard * standard, 0, keepdims=True)
        - jnp.log(spread)
        - 0.5 * math.log(2.0 * math.pi)
    )
    mean_ref[0] = next_mean


ANY = pl.BlockSpec(memory_space=pl.ANY)
VMEM = pl.BlockSpec(memory_space=pltpu.VMEM)
SMEM = pl.BlockSpec(memory_space=pltpu.SMEM)
work = [
    pltpu.VMEM((TPF, D), bf16),
    pltpu.VMEM((TPF, 2 * D), f32),
    pltpu.VMEM((TPF, 3 * D), bf16),
    pltpu.VMEM((TPF, D), bf16),
]


def shards(
    hidden,
    latents_now,
    latents_next,
    timestep,
    version_tags,
    noise_levels,
    time_weight,
    spatial_qkv,
    spatial_out,
    temporal_qkv,
    temporal_out,
    final_weight,
):
    after_spatial, table = pl.pallas_call(
        spatial_kernel,
        out_shape=(
            jax.ShapeDtypeStruct((TPF, D), bf16),
            jax.ShapeDtypeStruct((8, 3 * D), f32),
        ),
        in_specs=[SMEM, ANY, ANY, ANY, ANY],
        out_specs=(VMEM, VMEM),
        scratch_shapes=[
            pltpu.VMEM((TPF, D), bf16),
            pltpu.VMEM((FREQ, 6 * D), bf16),
            pltpu.VMEM((D, 3 * D), bf16),
            pltpu.VMEM((D, D), bf16),
            pltpu.VMEM((2 * D, LANES), bf16),
            *work,
            pltpu.SemaphoreType.DMA((4 + len(CHUNKS),)),
        ],
        compiler_params=pltpu.CompilerParams(vmem_limit_bytes=32 << 20),
        name="spatial",
    )(timestep, hidden, time_weight, spatial_qkv, spatial_out)
    peers = lax.axis_size(("inner", "outer"))
    per_peer = TPF // peers
    blocks = after_spatial.reshape(peers, per_peer, D)
    arrived = lax.all_to_all(blocks, ("inner", "outer"), split_axis=0, concat_axis=0, tiled=True)
    velocity = pl.pallas_call(
        temporal_kernel,
        out_shape=jax.ShapeDtypeStruct((TPF, LANES), f32),
        in_specs=[VMEM] * 5,
        out_specs=VMEM,
        scratch_shapes=[
            pltpu.VMEM((2 * D, LANES), bf16),
            pltpu.VMEM((TPF, TPF), bf16),
            *work,
            pltpu.VMEM((TPF, D), bf16),
        ],
        compiler_params=pltpu.CompilerParams(vmem_limit_bytes=32 << 20),
        name="temporal",
    )(arrived.reshape(TPF, D), table, temporal_qkv, temporal_out, final_weight)
    returned = lax.all_to_all(
        velocity.reshape(peers, per_peer, LANES),
        ("inner", "outer"),
        split_axis=0,
        concat_axis=0,
        tiled=True,
    )
    return pl.pallas_call(
        density_kernel,
        out_shape=(
            jax.ShapeDtypeStruct((1, TPF), f32),
            jax.ShapeDtypeStruct((1, C, TPF), f32),
        ),
        in_specs=[SMEM, SMEM, SMEM, VMEM, VMEM, VMEM],
        out_specs=(VMEM, VMEM),
        name="density",
    )(
        timestep, version_tags, noise_levels, returned.reshape(TPF, LANES), latents_now, latents_next
    )


def solution(mesh):
    return jax.shard_map(
        shards,
        mesh=mesh,
        in_specs=(
            P(("inner", "outer"), None),
            P(("inner", "outer"), None, None),
            P(("inner", "outer"), None, None),
            P(),
            P(("inner", "outer")),
            P(),
            P(),
            P(),
            P(),
            P(),
            P(),
            P(),
        ),
        out_specs=(P(("inner", "outer"), None), P(("inner", "outer"), None, None)),
        check_vma=False,
    )
```

time: 145 us -> 84.2 us (0.58)
  local copies, waits for them, and re-layouts: 48.9 us -> 15 us
  Pallas kernels: 0 us -> 26.9 us
  other arithmetic: 20.4 us -> 0 us
  matrix products: 16.9 us -> 0 us
  blocking collectives: 38 us -> 25.7 us
  waiting for transfers between devices: 11.9 us -> 9.24 us
    pallas_call x0 -> x3, Pallas kernels: none -> 26.9 us  [the longest x1 12.8 us: shards(): pl.pallas_call(spatial_kernel, out_shape=(jax.ShapeDtypeStruct((TPF, D),...]
    mul x12 -> x0, local copies, waits for them, and re-layouts: 25.6 us -> none  [the longest x8 15 us: head_norm(): values * lax.rsqrt(jnp.mean(values * values, -1, keepdims=True) + norm_eps)]
    dot_general x10 -> x0, matrix products: 16.9 us -> none  [the longest x2 8.73 us: project_rows(): mixed = jnp.dot(normed, qkv_weight, preferred_element_type=jnp.float32)]
    all_to_all x1, blocking collectives: 38 us -> 25.7 us  [shards(): lax.all_to_all(blocks, ('inner', 'outer'), split_axis=0, concat_axis=0, t...]
    slice x9 -> x0, local copies, waits for them, and re-layouts: 9.89 us -> none  [the longest x3 3.88 us: project_rows(): mixed[:, 2 * D:]]
    unnamed x44 -> x16, local copies, waits for them, and re-layouts: 4.31 us -> 12 us
    reduce_sum x10 -> x0, other arithmetic: 7.29 us -> none  [the longest x4 5.47 us: head_norm(): jnp.mean(values * values, -1, keepdims=True) + norm_eps]
    concatenate x3 -> x0, local copies, waits for them, and re-layouts: 5.67 us -> none  [project_rows(): jnp.concatenate([queries.reshape(rows, D), key_rows.reshape(rows, D), mix...]
where the time goes in v1:
time: 84.2 us; the launch traced here: 83.7 us
  Pallas kernels  26.9 us (32%)
  blocking collectives  25.7 us (31%)
  local copies, waits for them, and re-layouts  15 us (18%)
  waiting for transfers between devices  9.24 us (11%)
  starting transfers between devices  4.84 us (6%)
  between operations  2 us (2%)
    all_to_all x1, blocking collectives, shards(): lax.all_to_all(blocks, ('inner', 'outer'), split_axis=0, concat_axis=0, t...  25.7 us
    pallas_call x1, Pallas kernels, shards(): pl.pallas_call(spatial_kernel, out_shape=(jax.ShapeDtypeStruct((TPF, D),...  12.8 us
    pallas_call x1, Pallas kernels, shards(): pl.pallas_call(temporal_kernel, out_shape=jax.ShapeDtypeStruct((TPF, LANE...  12.5 us
    unnamed x16, local copies, waits for them, and re-layouts  12 us
    all_to_all x1, waiting for transfers between devices, shards(): lax.all_to_all(velocity.reshape(peers, per_peer, LANES), ('inner', 'outer...  9.24 us
    all_to_all x1, starting transfers between devices, shards(): lax.all_to_all(velocity.reshape(peers, per_peer, LANES), ('inner', 'outer...  4.84 us
    reshape x1, local copies, waits for them, and re-layouts, shards(): arrived.reshape(TPF, D)  1.98 us
  transfers between devices with their start and end apart: 1, of which 1 were waited for; matrix products, arithmetic and copies ran while one was open for 0% of the time, Pallas kernels for 0%

profile of v1, /device:TPU:1, one launch (start us, length us, event | category | flops | bytes accessed | tf_op | source)
XLA Modules:
  0.0 83.7 jit_solution(17593760937142104420)
XLA Ops:
  1.3 0.0 copy-start
  1.3 3.3 %copy-done = bf16[1152,3456]{1,0:T(8,128)(2,1)S(1)} copy-done((bf16[1152,3456]{1,0:T(8,128)(2,1)S(1)}, bf16[1152,3456]{1,0:T(8,128)(2,1)}, u32[]{:S(2)}) %copy-start) | copy-done | bytes 7962648
  4.5 0.0 copy-start.2
  4.5 2.0 %copy-done.2 = bf16[256,6912]{1,0:T(8,128)(2,1)S(1)} copy-done((bf16[256,6912]{1,0:T(8,128)(2,1)S(1)}, bf16[256,6912]{1,0:T(8,128)(2,1)}, u32[]{:S(2)}) %copy-start.2) | copy-done | bytes 3538968
  6.5 0.0 copy-start.3
  6.5 1.7 %copy-done.3 = bf16[1152,1152]{1,0:T(8,128)(2,1)S(1)} copy-done((bf16[1152,1152]{1,0:T(8,128)(2,1)S(1)}, bf16[1152,1152]{1,0:T(8,128)(2,1)}, u32[]{:S(2)}) %copy-start.3) | copy-done | bytes 2654232
  8.3 0.0 copy-start.5
  8.3 1.1 %copy-done.5 = bf16[256,1152]{1,0:T(8,128)(2,1)S(1)} copy-done((bf16[256,1152]{1,0:T(8,128)(2,1)S(1)}, bf16[256,1152]{1,0:T(8,128)(2,1)}, u32[]{:S(2)}) %copy-start.5) | copy-done | bytes 589848
  9.4 12.8 %spatial.1 = (bf16[256,1152]{1,0:T(8,128)(2,1)S(1)}, f32[8,3456]{1,0:T(8,128)S(1)}) custom-call(s32[1]{0:T(128)S(6)} %copy.14.step_ref, bf16[256,1152]{1,0:T(8,128)(2,1)S(1)} %copy-done.5, bf16[256,6912]{1,0:T(8,128)(2,1)S(1)} %copy-done.2, bf16[1152,3456]{1,0:T(8,128)(2,1)S(1)} %copy-done, bf16[1152,1152]{1,0:T(8,128)(2,1)S(1)} %copy-done.3), custom_call_target="tpu_custom_call" | custom-call | tf_op jit(solution)/shard_map/spatial/pallas_call | solution.py:253
  22.2 0.0 copy-start.4
  22.2 0.0 copy-start.6
  22.2 1.0 %reshape.16 = bf16[128,2,1152]{2,1,0:T(2,128)(2,1)} reshape(bf16[256,1152]{1,0:T(8,128)(2,1)S(1)} %get-tuple-element.4) | data formatting | bytes 1179648 | tf_op jit(solution)/shard_map/reshape | solution.py:275
  23.2 25.7 %all_to_all.10 = bf16[128,2,1152]{2,1,0:T(2,128)(2,1)} all-to-all(bf16[128,2,1152]{2,1,0:T(2,128)(2,1)} %reshape.16), channel_id=1, replica_groups=mesh['inner'=32,'outer'=4] {'inner','outer'}, dimensions={0} | all-to-all | bytes 1179648 | tf_op jit(solution)/shard_map/all_to_all | solution.py:276
  49.0 2.0 %reshape.17.after_ref = bf16[256,1152]{1,0:T(8,128)(2,1)S(1)} reshape(bf16[128,2,1152]{2,1,0:T(2,128)(2,1)} %all_to_all.10) | data formatting | bytes 1179648 | tf_op jit(solution)/shard_map/reshape | solution.py:290
  51.0 0.0 copy-done.4
  51.0 0.0 copy-done.6
  51.0 0.0 copy-start.1
  51.0 3.3 %copy-done.1 = bf16[1152,3456]{1,0:T(8,128)(2,1)S(1)} copy-done((bf16[1152,3456]{1,0:T(8,128)(2,1)S(1)}, bf16[1152,3456]{1,0:T(8,128)(2,1)}, u32[]{:S(2)}) %copy-start.1) | copy-done | bytes 7962648
  54.2 12.5 %temporal.1 = f32[256,128]{1,0:T(8,128)} custom-call(bf16[256,1152]{1,0:T(8,128)(2,1)S(1)} %reshape.17.after_ref, f32[8,3456]{1,0:T(8,128)S(1)} %get-tuple-element.5.table_ref, bf16[1152,3456]{1,0:T(8,128)(2,1)S(1)} %copy-done.1, bf16[1152,1152]{1,0:T(8,128)(2,1)S(1)} %copy-done.4, bf16[16,1152]{1,0:T(8,128)(2,1)S(1)} %copy-done.6), custom_call_target="tpu_custom_call" | custom-call | tf_op jit(solution)/shard_map/temporal/pallas_call | solution.py:277
  66.7 4.8 %all-to-all-start.1 = ((f32[128,2,128]{2,1,0:T(2,128)}), f32[128,2,128]{2,1,0:T(2,128)S(1)}, u32[]{:S(2)}, u32[]{:S(2)}) async-start(f32[128,2,128]{2,1,0:T(2,128)} %bitcast), calls=%async_computation.1 | async-start | bytes 262144 | tf_op jit(solution)/shard_map/all_to_all | solution.py:291
  72.2 9.2 %all-to-all-done.1 = f32[128,2,128]{2,1,0:T(2,128)S(1)} async-done(((f32[128,2,128]{2,1,0:T(2,128)}), f32[128,2,128]{2,1,0:T(2,128)S(1)}, u32[]{:S(2)}, u32[]{:S(2)}) %all-to-all-start.1) | async-done | bytes 131104 | tf_op jit(solution)/shard_map/all_to_all | solution.py:291
  81.5 0.0 copy-start.7
  81.5 0.6 copy-done.7
  82.1 1.6 %density.1 = (f32[1,256]{1,0:T(1,128)}, f32[1,16,256]{2,1,0:T(8,128)}) custom-call(s32[1]{0:T(128)S(6)} %copy.14.step_ref, s32[1]{0:T(128)S(6)} %copy.15.tag_ref, f32[8]{0:T(128)} %level_ref.1, f32[256,128]{1,0:T(8,128)} %bitcast.2, f32[1,16,256]{2,1,0:T(8,128)} %now_ref.1, f32[1,16,256]{2,1,0:T(8,128)} %next_ref.1), custom_call_target="tpu_custom_call" | custom-call | tf_op jit(solution)/shard_map/density/pallas_call | solution.py:298
Async XLA Ops:
  1.3 3.3 %copy-start = (bf16[1152,3456]{1,0:T(8,128)(2,1)S(1)}, bf16[1152,3456]{1,0:T(8,128)(2,1)}, u32[]{:S(2)}) copy-start(bf16[1152,3456]{1,0:T(8,128)(2,1)} %qkv_hbm.1) | copy-start | bytes 23887876
  4.5 2.0 %copy-start.2 = (bf16[256,6912]{1,0:T(8,128)(2,1)S(1)}, bf16[256,6912]{1,0:T(8,128)(2,1)}, u32[]{:S(2)}) copy-start(bf16[256,6912]{1,0:T(8,128)(2,1)} %time_hbm.1) | copy-start | bytes 10616836
  6.5 1.7 %copy-start.3 = (bf16[1152,1152]{1,0:T(8,128)(2,1)S(1)}, bf16[1152,1152]{1,0:T(8,128)(2,1)}, u32[]{:S(2)}) copy-start(bf16[1152,1152]{1,0:T(8,128)(2,1)} %out_hbm.1) | copy-start | bytes 7962628
  8.3 1.1 %copy-start.5 = (bf16[256,1152]{1,0:T(8,128)(2,1)S(1)}, bf16[256,1152]{1,0:T(8,128)(2,1)}, u32[]{:S(2)}) copy-start(bf16[256,1152]{1,0:T(8,128)(2,1)} %hidden_hbm.1) | copy-start | bytes 1769476
  22.2 28.8 %copy-start.4 = (bf16[1152,1152]{1,0:T(8,128)(2,1)S(1)}, bf16[1152,1152]{1,0:T(8,128)(2,1)}, u32[]{:S(2)}) copy-start(bf16[1152,1152]{1,0:T(8,128)(2,1)} %out_weight.1) | copy-start | bytes 7962628
  22.2 28.8 %copy-start.6 = (bf16[16,1152]{1,0:T(8,128)(2,1)S(1)}, bf16[16,1152]{1,0:T(8,128)(2,1)}, u32[]{:S(2)}) copy-start(bf16[16,1152]{1,0:T(8,128)(2,1)} %final_weight.1) | copy-start | bytes 110596
  51.0 3.3 %copy-start.1 = (bf16[1152,3456]{1,0:T(8,128)(2,1)S(1)}, bf16[1152,3456]{1,0:T(8,128)(2,1)}, u32[]{:S(2)}) copy-start(bf16[1152,3456]{1,0:T(8,128)(2,1)} %qkv.1) | copy-start | bytes 23887876
  66.7 14.7 %all-to-all-start.1 = ((f32[128,2,128]{2,1,0:T(2,128)}), f32[128,2,128]{2,1,0:T(2,128)S(1)}, u32[]{:S(2)}, u32[]{:S(2)}) async-start(f32[128,2,128]{2,1,0:T(2,128)} %bitcast), calls=%async_computation.1 | async-start | bytes 262144 | tf_op jit(solution)/shard_map/all_to_all | solution.py:291
  81.5 0.6 copy-start.7

commit v2 on v1

--- a/solution.py
+++ b/solution.py
@@ -17,7 +17,10 @@
 TPF = 256
 LANES = 128
 CHUNKS = tuple((low, min(512, 3 * D - low)) for low in range(0, 3 * D, 512))
+OUT_CHUNKS = tuple((low, min(512, D - low)) for low in range(0, D, 512))
 ROWS = 32
+SPATIAL_VMEM = 40 << 20
+PREPARE_VMEM = 8 << 20
 
 norm_eps = 1e-06
 f32 = jnp.float32
@@ -51,7 +54,7 @@
         normed[rows, :] = (values * (1.0 + scale) + shift).astype(bf16)
         return carry
 
-    lax.fori_loop(0, TPF // ROWS, step, 0)
+    lax.fori_loop(0, TPF // ROWS, step, 0, unroll=True)
 
 
 def project(normed, weight, picker, raw, packed, ready):
@@ -89,17 +92,17 @@
 
 def attend(packed, attended, same):
     ones = jnp.ones((TPF, LANES), bf16)
+    lane = iota((TPF, LANES), 1)
+    pending = None
     for head in range(HEADS):
         start = head * HEAD
         low = start // LANES * LANES
         high = -(-(start + HEAD) // LANES) * LANES
-        width = high - low
-        lane = iota((TPF, width), 1) + low
-        inside = (lane >= start) & (lane < start + HEAD)
+        wide = iota((TPF, high - low), 1) + low
+        inside = (wide >= start) & (wide < start + HEAD)
         queries = packed[:, low:high]
-        queries = jnp.where(inside, queries, jnp.zeros_like(queries))
         scores = lax.dot_general(
-            queries,
+            jnp.where(inside, queries, jnp.zeros_like(queries)),
             packed[:, D + low : D + high],
             (((1,), (1,)), ((), ())),
             preferred_element_type=f32,
@@ -107,20 +110,35 @@
         weights = jnp.exp2(scores).astype(bf16)
         if same is not None:
             weights = weights * same[...]
-        total = jnp.dot(weights, ones, preferred_element_type=f32)
-        mixed = jnp.dot(weights, packed[:, 2 * D + low : 2 * D + high], preferred_element_type=f32)
-        share = 1.0 / total
-        for tile in range(low, high, LANES):
-            result = mixed[:, tile - low : tile - low + LANES] * share
-            if start > tile:
-                keep = iota((TPF, LANES), 1) + tile < start
-                result = jnp.where(keep, attended[:, tile : tile + LANES].astype(f32), result)
-            attended[:, tile : tile + LANES] = result.astype(bf16)
+        values = packed[:, 2 * D + low : 2 * D + high]
+        single = high - low == LANES
+        if single:
+            values = jnp.concatenate([values, ones], 1)
+        else:
+            values = jnp.where(inside, values, jnp.ones_like(values))
+        mixed = jnp.dot(weights, values, preferred_element_type=f32)
+        left, right = mixed[:, :LANES], mixed[:, LANES:]
+        before = lane < start - low
+        share = 1.0 / (right if single else jnp.where(before, left, right))
+        left = left * share
+        if start > low:
+            left = jnp.where(before, pending, left)
+        pending = left if single else right * share
+        if start + HEAD >= low + LANES:
+            attended[:, low : low + LANES] = left.astype(bf16)
+
+
+def embed(step_ref):
+    time_value = jnp.full((16, FREQ // 2), step_ref[0], jnp.int32).astype(f32) / STEPS
+    position = iota((16, FREQ // 2), 1).astype(f32)
+    angles = 1000.0 * time_value * jnp.exp(-math.log(10000.0) * position / (FREQ // 2))
+    embedded = jnp.concatenate([jnp.cos(angles), jnp.sin(angles)], 1)
+    return (embedded / (1.0 + jnp.exp(-embedded))).astype(bf16)
 
 
 def spatial_kernel(
     step_ref, hidden_hbm, time_hbm, qkv_hbm, out_hbm,
-    after_ref, table_ref,
+    after_ref,
     hidden, time_weight, qkv, out_weight, picker, normed, raw, packed, attended, sems,
 ):
     copies = [pltpu.make_async_copy(hidden_hbm, hidden, sems.at[0])]
@@ -136,22 +154,17 @@
             )
         )
     last = 2 + len(CHUNKS)
-    copies.append(pltpu.make_async_copy(out_hbm, out_weight, sems.at[last]))
     copies.append(
         pltpu.make_async_copy(
-            time_hbm.at[:, 2 * D : 6 * D], time_weight.at[:, 2 * D : 6 * D], sems.at[last + 1]
-        )
-    )
+            time_hbm.at[:, 2 * D : 3 * D], time_weight.at[:, 2 * D : 3 * D], sems.at[last]
+        )
+    )
+    copies.append(pltpu.make_async_copy(out_hbm, out_weight, sems.at[last + 1]))
     for copy in copies:
         copy.start()
 
     fill_picker(picker)
-    time_value = jnp.full((16, FREQ // 2), step_ref[0], jnp.int32).astype(f32) / STEPS
-    position = iota((16, FREQ // 2), 1).astype(f32)
-    angles = 1000.0 * time_value * jnp.exp(-math.log(10000.0) * position / (FREQ // 2))
-    embedded = jnp.concatenate([jnp.cos(angles), jnp.sin(angles)], 1)
-    activated = (embedded / (1.0 + jnp.exp(-embedded))).astype(bf16)
-
+    activated = embed(step_ref)
     copies[0].wait()
     copies[1].wait()
     first = jnp.dot(activated, time_weight[:, 0 : 2 * D], preferred_element_type=f32)
@@ -159,45 +172,79 @@
     project(normed, qkv, picker, raw, packed, lambda index: copies[2 + index].wait())
     attend(packed, attended, None)
     copies[last].wait()
+    gate = jnp.dot(activated, time_weight[:, 2 * D : 3 * D], preferred_element_type=f32)[0:1, :]
     copies[last + 1].wait()
-    rest = jnp.dot(activated, time_weight[:, 2 * D : 6 * D], preferred_element_type=f32)
-    table_ref[...] = rest[0:8, D:]
-    gate = rest[0:1, 0:D]
-    for low in range(0, D, 256):
-        width = min(256, D - low)
+    for low, width in OUT_CHUNKS:
         projected = jnp.dot(
             attended[...], out_weight[:, low : low + width], preferred_element_type=f32
         )
-        after_ref[:, low : low + width] = (
-            hidden[:, low : low + width].astype(f32) + gate[:, low : low + width] * projected
-        ).astype(bf16)
-
-
-def temporal_kernel(
-    after_ref, table_ref, qkv, out_weight, final_weight,
-    velocity_ref,
-    picker, same, normed, raw, packed, attended, term,
+        after = hidden[:, low : low + width].astype(f32) + gate[:, low : low + width] * projected
+        after_ref[:, :, low : low + width] = after.astype(bf16).reshape(TPF // 2, 2, width)
+
+
+def prepare_kernel(
+    step_ref, time_hbm, table_hbm, picker_hbm, same_hbm, time_weight, table, picker, same, sems
 ):
+    copy = pltpu.make_async_copy(time_hbm.at[:, 3 * D : 6 * D], time_weight, sems.at[0])
+    copy.start()
     fill_picker(picker)
     parity = (iota((TPF, TPF), 0) ^ iota((TPF, TPF), 1)) & 1
     same[...] = jnp.where(parity == 0, 1.0, 0.0).astype(bf16)
-    modulate_rows(after_ref, table_ref[0:1, D : 2 * D], table_ref[0:1, 0:D], normed)
-    project(normed, qkv, picker, raw, packed, lambda index: None)
+    activated = embed(step_ref)
+    copy.wait()
+    table[...] = jnp.dot(activated, time_weight[...], preferred_element_type=f32)[0:8]
+    copies = [
+        pltpu.make_async_copy(source, target, sems.at[1 + index])
+        for index, (source, target) in enumerate(
+            ((table, table_hbm), (picker, picker_hbm), (same, same_hbm))
+        )
+    ]
+    for copy in copies:
+        copy.start()
+    for copy in copies:
+        copy.wait()
+
+
+def temporal_kernel(
+    arrived_ref, table_hbm, picker_hbm, same_hbm, qkv_hbm, out_hbm, final_hbm,
+    velocity_ref,
+    table, picker, same, qkv, out_weight, final_weight,
+    normed, raw, packed, attended, term, after, sems,
+):
+    pairs = [(table_hbm, table), (picker_hbm, picker)]
+    for low, width in CHUNKS:
+        pairs.append((qkv_hbm.at[:, low : low + width], qkv.at[:, low : low + width]))
+    last = len(pairs)
+    pairs += [(same_hbm, same), (out_hbm, out_weight), (final_hbm, final_weight)]
+    copies = [
+        pltpu.make_async_copy(source, target, sems.at[index])
+        for index, (source, target) in enumerate(pairs)
+    ]
+    for copy in copies:
+        copy.start()
+
+    after[...] = arrived_ref[...].reshape(TPF, D)
+    copies[0].wait()
+    modulate_rows(after, table[0:1, D : 2 * D], table[0:1, 0:D], normed)
+    copies[1].wait()
+    project(normed, qkv, picker, raw, packed, lambda index: copies[2 + index].wait())
+    copies[last].wait()
     attend(packed, attended, same)
-    for low in range(0, D, 256):
-        width = min(256, D - low)
+    copies[last + 1].wait()
+    for low, width in OUT_CHUNKS:
         term[:, low : low + width] = jnp.dot(
             attended[...], out_weight[:, low : low + width], preferred_element_type=f32
         ).astype(bf16)
-    gate = table_ref[0:1, 2 * D : 3 * D]
+    gate = table[0:1, 2 * D : 3 * D]
 
     def step(index, carry):
         rows = pl.ds(pl.multiple_of(index * ROWS, ROWS), ROWS)
-        state = after_ref[rows, :].astype(f32) + gate * term[rows, :].astype(f32)
+        state = after[rows, :].astype(f32) + gate * term[rows, :].astype(f32)
         normed[rows, :] = centre(state).astype(bf16)
         return carry
 
-    lax.fori_loop(0, TPF // ROWS, step, 0)
+    lax.fori_loop(0, TPF // ROWS, step, 0, unroll=True)
+    copies[last + 2].wait()
     velocity_ref[:, 0:C] = lax.dot_general(
         normed[...], final_weight[...], (((1,), (1,)), ((), ())), preferred_element_type=f32
     )
@@ -225,7 +272,7 @@
     mean_ref[0] = next_mean
 
 
-ANY = pl.BlockSpec(memory_space=pl.ANY)
+HBM = pl.BlockSpec(memory_space=pltpu.HBM)
 VMEM = pl.BlockSpec(memory_space=pltpu.VMEM)
 SMEM = pl.BlockSpec(memory_space=pltpu.SMEM)
 work = [
@@ -234,6 +281,10 @@
     pltpu.VMEM((TPF, 3 * D), bf16),
     pltpu.VMEM((TPF, D), bf16),
 ]
+
+
+def in_hbm(array):
+    return pltpu.with_memory_space_constraint(array, pltpu.HBM)
 
 
 def shards(
@@ -250,46 +301,85 @@
     temporal_out,
     final_weight,
 ):
-    after_spatial, table = pl.pallas_call(
+    time_weight = in_hbm(time_weight)
+    after_spatial = pl.pallas_call(
         spatial_kernel,
-        out_shape=(
-            jax.ShapeDtypeStruct((TPF, D), bf16),
-            jax.ShapeDtypeStruct((8, 3 * D), f32),
-        ),
-        in_specs=[SMEM, ANY, ANY, ANY, ANY],
-        out_specs=(VMEM, VMEM),
+        out_shape=jax.ShapeDtypeStruct((TPF // 2, 2, D), bf16),
+        in_specs=[SMEM, HBM, HBM, HBM, HBM],
+        out_specs=VMEM,
         scratch_shapes=[
             pltpu.VMEM((TPF, D), bf16),
-            pltpu.VMEM((FREQ, 6 * D), bf16),
+            pltpu.VMEM((FREQ, 3 * D), bf16),
             pltpu.VMEM((D, 3 * D), bf16),
             pltpu.VMEM((D, D), bf16),
             pltpu.VMEM((2 * D, LANES), bf16),
             *work,
             pltpu.SemaphoreType.DMA((4 + len(CHUNKS),)),
         ],
-        compiler_params=pltpu.CompilerParams(vmem_limit_bytes=32 << 20),
+        compiler_params=pltpu.CompilerParams(vmem_limit_bytes=SPATIAL_VMEM),
+        cost_estimate=pl.CostEstimate(
+            flops=4 << 30, bytes_accessed=14 << 20, transcendentals=1 << 20
+        ),
         name="spatial",
-    )(timestep, hidden, time_weight, spatial_qkv, spatial_out)
-    peers = lax.axis_size(("inner", "outer"))
-    per_peer = TPF // peers
-    blocks = after_spatial.reshape(peers, per_peer, D)
-    arrived = lax.all_to_all(blocks, ("inner", "outer"), split_axis=0, concat_axis=0, tiled=True)
+    )(timestep, in_hbm(hidden), time_weight, in_hbm(spatial_qkv), in_hbm(spatial_out))
+    arrived = lax.all_to_all(
+        after_spatial, ("inner", "outer"), split_axis=0, concat_axis=0, tiled=True
+    )
+    table, picker, same = pl.pallas_call(
+        prepare_kernel,
+        out_shape=(
+            jax.ShapeDtypeStruct((8, 3 * D), f32),
+            jax.ShapeDtypeStruct((2 * D, LANES), bf16),
+            jax.ShapeDtypeStruct((TPF, TPF), bf16),
+        ),
+        in_specs=[SMEM, HBM],
+        out_specs=(HBM, HBM, HBM),
+        scratch_shapes=[
+            pltpu.VMEM((FREQ, 3 * D), bf16),
+            pltpu.VMEM((8, 3 * D), f32),
+            pltpu.VMEM((2 * D, LANES), bf16),
+            pltpu.VMEM((TPF, TPF), bf16),
+            pltpu.SemaphoreType.DMA((4,)),
+        ],
+        compiler_params=pltpu.CompilerParams(vmem_limit_bytes=PREPARE_VMEM),
+        cost_estimate=pl.CostEstimate(
+            flops=32 << 20, bytes_accessed=3 << 20, transcendentals=1 << 13
+        ),
+        name="prepare",
+    )(timestep, time_weight)
     velocity = pl.pallas_call(
         temporal_kernel,
         out_shape=jax.ShapeDtypeStruct((TPF, LANES), f32),
-        in_specs=[VMEM] * 5,
+        in_specs=[VMEM] + [HBM] * 6,
         out_specs=VMEM,
         scratch_shapes=[
+            pltpu.VMEM((8, 3 * D), f32),
             pltpu.VMEM((2 * D, LANES), bf16),
             pltpu.VMEM((TPF, TPF), bf16),
+            pltpu.VMEM((D, 3 * D), bf16),
+            pltpu.VMEM((D, D), bf16),
+            pltpu.VMEM((C, D), bf16),
             *work,
             pltpu.VMEM((TPF, D), bf16),
+            pltpu.VMEM((TPF, D), bf16),
+            pltpu.SemaphoreType.DMA((5 + len(CHUNKS),)),
         ],
-        compiler_params=pltpu.CompilerParams(vmem_limit_bytes=32 << 20),
+        compiler_params=pltpu.CompilerParams(vmem_limit_bytes=40 << 20),
+        cost_estimate=pl.CostEstimate(
+            flops=4 << 30, bytes_accessed=12 << 20, transcendentals=1 << 20
+        ),
         name="temporal",
-    )(arrived.reshape(TPF, D), table, temporal_qkv, temporal_out, final_weight)
+    )(
+        arrived,
+        table,
+        picker,
+        same,
+        in_hbm(temporal_qkv),
+        in_hbm(temporal_out),
+        in_hbm(final_weight),
+    )
     returned = lax.all_to_all(
-        velocity.reshape(peers, per_peer, LANES),
+        velocity.reshape(TPF // 2, 2, LANES),
         ("inner", "outer"),
         split_axis=0,
         concat_axis=0,
@@ -303,6 +393,7 @@
         ),
         in_specs=[SMEM, SMEM, SMEM, VMEM, VMEM, VMEM],
         out_specs=(VMEM, VMEM),
+        compiler_params=pltpu.CompilerParams(vmem_limit_bytes=4 << 20),
         name="density",
     )(
         timestep, version_tags, noise_levels, returned.reshape(TPF, LANES), latents_now, latents_next

time: 84.2 us -> 63 us (0.75)
  blocking collectives: 25.7 us -> 0 us
  local copies, waits for them, and re-layouts: 15 us -> 0.01 us
  waiting for transfers between devices: 9.24 us -> 21.1 us
  starting transfers between devices: 4.84 us -> 16.4 us
  Pallas kernels: 26.9 us -> 23.3 us
    all_to_all x1 -> x0, blocking collectives: 25.7 us -> none  [shards(): lax.all_to_all(blocks, ('inner', 'outer'), split_axis=0, concat_axis=0, t...]
    unnamed x16 -> x6, local copies, waits for them, and re-layouts: 12 us -> 0.01 us
    all_to_all x1 -> x2, waiting for transfers between devices: 9.24 us -> 21.1 us  [the longest x1 11.8 us: shards(): lax.all_to_all(after_spatial, ('inner', 'outer'), split_axis=0, concat_ax...]
    all_to_all x1 -> x2, starting transfers between devices: 4.84 us -> 16.4 us  [the longest x1 11.5 us: shards(): lax.all_to_all(after_spatial, ('inner', 'outer'), split_axis=0, concat_ax...]
    reshape x2 -> x0, local copies, waits for them, and re-layouts: 3.01 us -> none  [the longest x1 1.98 us: shards(): arrived.reshape(TPF, D)]
    pallas_call x1, Pallas kernels: 12.5 us -> 10 us  [shards(): pl.pallas_call(temporal_kernel, out_shape=jax.ShapeDtypeStruct((TPF, LANE...]
    pallas_call x1 -> x2, Pallas kernels: 12.8 us -> 12.1 us  [the longest x1 9.8 us: shards(): pl.pallas_call(spatial_kernel, out_shape=jax.ShapeDtypeStruct((TPF // 2,...]
  transfers between devices with their start and end apart: 1 -> 2, of which waited for: 1 -> 2; matrix products, arithmetic and copies ran while one was open for 0% -> 0% of each run, Pallas kernels for 0% -> 4%
where the time goes in v2:
time: 63 us; the launch traced here: 62.8 us
  Pallas kernels  23.3 us (37%)
  waiting for transfers between devices  21.1 us (33%)
  starting transfers between devices  16.4 us (26%)
  between operations  1.97 us (3%)
    all_to_all x1, waiting for transfers between devices, shards(): lax.all_to_all(after_spatial, ('inner', 'outer'), split_axis=0, concat_ax...  11.8 us
    all_to_all x1, starting transfers between devices, shards(): lax.all_to_all(after_spatial, ('inner', 'outer'), split_axis=0, concat_ax...  11.5 us
    pallas_call x1, Pallas kernels, shards(): pl.pallas_call(temporal_kernel, out_shape=jax.ShapeDtypeStruct((TPF, LANE...  10 us
    pallas_call x1, Pallas kernels, shards(): pl.pallas_call(spatial_kernel, out_shape=jax.ShapeDtypeStruct((TPF // 2,...  9.8 us
    all_to_all x1, waiting for transfers between devices, shards(): lax.all_to_all(velocity.reshape(TPF // 2, 2, LANES), ('inner', 'outer'),...  9.25 us
    all_to_all x1, starting transfers between devices, shards(): lax.all_to_all(velocity.reshape(TPF // 2, 2, LANES), ('inner', 'outer'),...  4.86 us
    pallas_call x1, Pallas kernels, shards(): pl.pallas_call(prepare_kernel, out_shape=(jax.ShapeDtypeStruct((8, 3 * D)...  2.27 us
  transfers between devices with their start and end apart: 2, of which 2 were waited for; matrix products, arithmetic and copies ran while one was open for 0% of the time, Pallas kernels for 4%

profile of v2, /device:TPU:1, one launch (start us, length us, event | category | flops | bytes accessed | tf_op | source)
XLA Modules:
  0.0 62.8 jit_solution(7892853066306458363)
XLA Ops:
  1.3 9.8 %spatial.1 = bf16[128,2,1152]{2,1,0:T(2,128)(2,1)} custom-call(s32[1]{0:T(128)S(6)} %copy.14.step_ref, bf16[256,1152]{1,0:T(8,128)(2,1)} %hidden_hbm.1, bf16[256,6912]{1,0:T(8,128)(2,1)} %time_hbm.3, bf16[1152,3456]{1,0:T(8,128)(2,1)} %qkv_hbm.2, bf16[1152,1152]{1,0:T(8,128)(2,1)} %out_hbm.2), custom_call_target="tpu_custom_call" | custom-call | flops 4294967296 | bytes 14680064 | tf_op jit(solution)/shard_map/spatial/pallas_call | solution.py:305
  11.1 11.5 %all-to-all-start = ((bf16[128,2,1152]{2,1,0:T(2,128)(2,1)}), bf16[128,2,1152]{2,1,0:T(2,128)(2,1)S(1)}, u32[]{:S(2)}, u32[]{:S(2)}) async-start(bf16[128,2,1152]{2,1,0:T(2,128)(2,1)} %spatial.1), calls=%async_computation | async-start | bytes 1179648 | tf_op jit(solution)/shard_map/all_to_all | solution.py:325
  22.6 2.3 %prepare.1 = (f32[8,3456]{1,0:T(8,128)S(1)}, bf16[2304,128]{1,0:T(8,128)(2,1)S(1)}, bf16[256,256]{1,0:T(8,128)(2,1)S(1)}) custom-call(s32[1]{0:T(128)S(6)} %copy.14.step_ref, bf16[256,6912]{1,0:T(8,128)(2,1)} %time_hbm.3), custom_call_target="tpu_custom_call" | custom-call | flops 33554432 | bytes 3145728 | tf_op jit(solution)/shard_map/prepare/pallas_call | solution.py:328
  24.9 11.8 %all-to-all-done.arrived_ref = bf16[128,2,1152]{2,1,0:T(2,128)(2,1)S(1)} async-done(((bf16[128,2,1152]{2,1,0:T(2,128)(2,1)}), bf16[128,2,1152]{2,1,0:T(2,128)(2,1)S(1)}, u32[]{:S(2)}, u32[]{:S(2)}) %all-to-all-start) | async-done | bytes 589856 | tf_op jit(solution)/shard_map/all_to_all | solution.py:325
  36.7 0.0 copy-start
  36.7 0.0 copy-start.1
  36.7 0.0 copy-start.2
  36.7 10.0 %temporal.1 = f32[256,128]{1,0:T(8,128)} custom-call(bf16[128,2,1152]{2,1,0:T(2,128)(2,1)S(1)} %all-to-all-done.arrived_ref, f32[8,3456]{1,0:T(8,128)S(1)} %get-tuple-element.5.table_hbm, bf16[2304,128]{1,0:T(8,128)(2,1)S(1)} %get-tuple-element.6.picker_hbm, bf16[256,256]{1,0:T(8,128)(2,1)S(1)} %get-tuple-element.7.same_hbm, bf16[1152,3456]{1,0:T(8,128)(2,1)} %qkv_hbm.3, ...), custom_call_target="tpu_custom_call" | custom-call | flops 4294967296 | bytes 12582912 | tf_op jit(solution)/shard_map/temporal/pallas_call | solution.py:350
  46.8 4.9 %all-to-all-start.1 = ((f32[128,2,128]{2,1,0:T(2,128)}), f32[128,2,128]{2,1,0:T(2,128)S(1)}, u32[]{:S(2)}, u32[]{:S(2)}) async-start(f32[128,2,128]{2,1,0:T(2,128)} %bitcast), calls=%async_computation.1 | async-start | bytes 262144 | tf_op jit(solution)/shard_map/all_to_all | solution.py:381
  52.3 9.3 %all-to-all-done.1 = f32[128,2,128]{2,1,0:T(2,128)S(1)} async-done(((f32[128,2,128]{2,1,0:T(2,128)}), f32[128,2,128]{2,1,0:T(2,128)S(1)}, u32[]{:S(2)}, u32[]{:S(2)}) %all-to-all-start.1) | async-done | bytes 131104 | tf_op jit(solution)/shard_map/all_to_all | solution.py:381
  61.5 0.0 copy-done
  61.5 0.0 copy-done.1
  61.5 0.0 copy-done.2
  61.5 1.2 %density.1 = (f32[1,256]{1,0:T(1,128)}, f32[1,16,256]{2,1,0:T(8,128)}) custom-call(s32[1]{0:T(128)S(6)} %copy.14.step_ref, s32[1]{0:T(128)S(6)} %copy.15.tag_ref, f32[8]{0:T(128)S(1)} %copy-done.2, f32[256,128]{1,0:T(8,128)S(1)} %bitcast.2, f32[1,16,256]{2,1,0:T(8,128)S(1)} %copy-done, f32[1,16,256]{2,1,0:T(8,128)S(1)} %copy-done.1), custom_call_target="tpu_custom_call" | custom-call | tf_op jit(solution)/shard_map/density/pallas_call | solution.py:388
Async XLA Ops:
  11.1 25.6 %all-to-all-start = ((bf16[128,2,1152]{2,1,0:T(2,128)(2,1)}), bf16[128,2,1152]{2,1,0:T(2,128)(2,1)S(1)}, u32[]{:S(2)}, u32[]{:S(2)}) async-start(bf16[128,2,1152]{2,1,0:T(2,128)(2,1)} %spatial.1), calls=%async_computation | async-start | bytes 1179648 | tf_op jit(solution)/shard_map/all_to_all | solution.py:325
  36.7 24.8 %copy-start = (f32[1,16,256]{2,1,0:T(8,128)S(1)}, f32[1,16,256]{2,1,0:T(8,128)}, u32[]{:S(2)}) copy-start(f32[1,16,256]{2,1,0:T(8,128)} %now_ref.1) | copy-start | bytes 49156
  36.7 24.8 %copy-start.1 = (f32[1,16,256]{2,1,0:T(8,128)S(1)}, f32[1,16,256]{2,1,0:T(8,128)}, u32[]{:S(2)}) copy-start(f32[1,16,256]{2,1,0:T(8,128)} %next_ref.1) | copy-start | bytes 49156
  36.7 24.8 %copy-start.2 = (f32[8]{0:T(128)S(1)}, f32[8]{0:T(128)}, u32[]{:S(2)}) copy-start(f32[8]{0:T(128)} %level_ref.1) | copy-start | bytes 100
  46.8 14.8 %all-to-all-start.1 = ((f32[128,2,128]{2,1,0:T(2,128)}), f32[128,2,128]{2,1,0:T(2,128)S(1)}, u32[]{:S(2)}, u32[]{:S(2)}) async-start(f32[128,2,128]{2,1,0:T(2,128)} %bitcast), calls=%async_computation.1 | async-start | bytes 262144 | tf_op jit(solution)/shard_map/all_to_all | solution.py:381

commit v3 on v2

v3 whole, which is shorter than its diff:
```python
import math

import jax
import jax.numpy as jnp
from jax import lax
from jax.experimental import pallas as pl
from jax.experimental.pallas import tpu as pltpu
from jax.sharding import PartitionSpec as P

D = 1152
HEADS = 16
HEAD = D // HEADS
C = 16
FREQ = 256
STEPS = 10
VERSIONS = 8
TPF = 256
LANES = 128
OUT_CHUNKS = tuple((low, min(512, D - low)) for low in range(0, D, 512))
ROWS = 32

norm_eps = 1e-06
f32 = jnp.float32
bf16 = jnp.bfloat16


def iota(shape, dim):
    return lax.broadcasted_iota(jnp.int32, shape, dim)


def centre(values):
    centred = values - jnp.mean(values, -1, keepdims=True)
    variance = jnp.mean(centred * centred, -1, keepdims=True)
    return centred * lax.rsqrt(variance + norm_eps)


def fill_picker(picker):
    for low in range(0, 2 * D, 256):
        column = iota((256, LANES), 0) + low
        lane = iota((256, LANES), 1)
        head = jnp.where(lane < 2 * HEADS, lane, lane - 2 * HEADS)
        offset = column - head * HEAD
        inside = (offset >= 0) & (offset < HEAD) & (lane < 4 * HEADS)
        picker[low : low + 256, :] = jnp.where(inside, 1.0, 0.0).astype(bf16)


def by_rows(step):
    def one(index, carry):
        step(pl.ds(pl.multiple_of(index * ROWS, ROWS), ROWS))
        return carry

    lax.fori_loop(0, TPF // ROWS, one, 0, unroll=True)


def embed(step_ref):
    time_value = jnp.full((16, FREQ // 2), step_ref[0], jnp.int32).astype(f32) / STEPS
    position = iota((16, FREQ // 2), 1).astype(f32)
    angles = 1000.0 * time_value * jnp.exp(-math.log(10000.0) * position / (FREQ // 2))
    embedded = jnp.concatenate([jnp.cos(angles), jnp.sin(angles)], 1)
    return (embedded / (1.0 + jnp.exp(-embedded))).astype(bf16)


def copies_of(pairs, sems):
    copies = [
        pltpu.make_async_copy(source, target, sems.at[index])
        for index, (source, target) in enumerate(pairs)
    ]
    for copy in copies:
        copy.start()
    return copies


def project(normed, weights, picker, raw, packed, ready):
    def product(part):
        ready(part)
        return jnp.dot(normed[...], weights[part][...], preferred_element_type=f32)

    def square_sums(part):
        total = jnp.zeros((TPF, LANES), f32)
        for low, width in OUT_CHUNKS:
            span = slice(part * D + low, part * D + low + width)
            values = raw[:, span]
            total = total + jnp.dot(
                (values * values).astype(bf16), picker[span, :], preferred_element_type=f32
            )
        return total

    raw[:, 0:D] = product(0)
    raw[:, D : 2 * D] = product(1)
    squares = square_sums(0)
    packed[:, 2 * D : 3 * D] = product(2).astype(bf16)
    squares = squares + square_sums(1)
    lane = iota((TPF, LANES), 1)
    head = jnp.where(lane < 2 * HEADS, lane, lane - 2 * HEADS)
    factor = lax.rsqrt(squares * (1.0 / HEAD) + norm_eps)
    factor = factor * jnp.where(head < HEADS, HEAD ** (-0.5) * math.log2(math.e), 1.0)
    coarse = factor.astype(bf16)
    fine = (factor - coarse.astype(f32)).astype(bf16)
    both = jnp.where(lane < 2 * HEADS, coarse.astype(f32), fine.astype(f32)).astype(bf16)
    for low in range(0, 2 * D, 256):
        spread = lax.dot_general(
            both,
            picker[low : low + 256, :],
            (((1,), (1,)), ((), ())),
            preferred_element_type=f32,
        )
        packed[:, low : low + 256] = (raw[:, low : low + 256] * spread).astype(bf16)


def attend(packed, attended, same):
    ones = jnp.ones((TPF, LANES), bf16)
    lane = iota((TPF, LANES), 1)
    pending = None
    for head in range(HEADS):
        start = head * HEAD
        low = start // LANES * LANES
        high = -(-(start + HEAD) // LANES) * LANES
        wide = iota((TPF, high - low), 1) + low
        inside = (wide >= start) & (wide < start + HEAD)
        queries = packed[:, low:high]
        scores = lax.dot_general(
            jnp.where(inside, queries, jnp.zeros_like(queries)),
            packed[:, D + low : D + high],
            (((1,), (1,)), ((), ())),
            preferred_element_type=f32,
        )
        weights = jnp.exp2(scores).astype(bf16)
        if same is not None:
            weights = weights * same[...]
        values = packed[:, 2 * D + low : 2 * D + high]
        single = high - low == LANES
        if single:
            values = jnp.concatenate([values, ones], 1)
        else:
            values = jnp.where(inside, values, jnp.ones_like(values))
        mixed = jnp.dot(weights, values, preferred_element_type=f32)
        left, right = mixed[:, :LANES], mixed[:, LANES:]
        before = lane < start - low
        share = 1.0 / (right if single else jnp.where(before, left, right))
        left = left * share
        if start > low:
            left = jnp.where(before, pending, left)
        pending = left if single else right * share
        if start + HEAD >= low + LANES:
            attended[:, low : low + LANES] = left.astype(bf16)


def spatial_kernel(
    step_ref, hidden_hbm, time_hbm, qkv_hbm, out_hbm,
    after_ref,
    hidden, modulation, gate_weight, query, key, value, out_weight, picker, normed, raw,
    packed, attended, sems,
):
    parts = (query, key, value)
    pairs = [(hidden_hbm, hidden), (time_hbm.at[:, 0 : 2 * D], modulation)]
    pairs += [(qkv_hbm.at[:, part * D : (part + 1) * D], parts[part]) for part in range(3)]
    pairs += [(time_hbm.at[:, 2 * D : 3 * D], gate_weight), (out_hbm, out_weight)]
    copies = copies_of(pairs, sems)

    fill_picker(picker)
    activated = embed(step_ref)
    copies[0].wait()

    def normalise(rows):
        raw[rows, 0:D] = centre(hidden[rows, :].astype(f32))

    by_rows(normalise)
    copies[1].wait()
    table = jnp.dot(activated, modulation[...], preferred_element_type=f32)
    shift, scale = table[0:1, 0:D], 1.0 + table[0:1, D : 2 * D]

    def modulate(rows):
        normed[rows, :] = (raw[rows, 0:D] * scale + shift).astype(bf16)

    by_rows(modulate)
    project(normed, parts, picker, raw, packed, lambda part: copies[2 + part].wait())
    attend(packed, attended, None)
    copies[5].wait()
    copies[6].wait()
    gate = jnp.dot(activated, gate_weight[...], preferred_element_type=f32)[0:1, :]
    for low, width in OUT_CHUNKS:
        projected = jnp.dot(
            attended[...], out_weight[:, low : low + width], preferred_element_type=f32
        )
        after = hidden[:, low : low + width].astype(f32) + gate[:, low : low + width] * projected
        after_ref[:, :, low : low + width] = after.astype(bf16).reshape(TPF // 2, 2, width)


def prepare_kernel(
    step_ref, tag_ref, level_ref, time_hbm, qkv_hbm,
    table_hbm, query_hbm, terms_hbm,
    modulation, table, terms, sems,
):
    copies = copies_of(
        [
            (time_hbm.at[:, 3 * D : 6 * D], modulation),
            (qkv_hbm.at[:, 0:D], query_hbm),
        ],
        sems,
    )
    activated = embed(step_ref)
    level = jnp.full((8, LANES), level_ref[tag_ref[0]], f32)
    time_value = jnp.full((8, LANES), step_ref[0], jnp.int32).astype(f32) / STEPS
    noise_scale = level * jnp.sqrt(time_value / (1.0 - time_value))
    spread = noise_scale * math.sqrt(1.0 / STEPS)
    terms[0:8, :] = noise_scale * noise_scale / (2.0 * time_value)
    terms[8:16, :] = 1.0 - time_value
    terms[16:24, :] = spread
    terms[24:32, :] = -jnp.log(spread)
    copies[0].wait()
    table[...] = jnp.dot(activated, modulation[...], preferred_element_type=f32)[0:8]
    results = [
        pltpu.make_async_copy(table, table_hbm, sems.at[2]),
        pltpu.make_async_copy(terms, terms_hbm, sems.at[3]),
    ]
    for copy in results:
        copy.start()
    for copy in results:
        copy.wait()
    copies[1].wait()


def temporal_kernel(
    arrived_ref, table, query, qkv_hbm, out_hbm, final_hbm,
    velocity_ref,
    picker, same, key, value, out_weight, final_weight,
    normed, raw, packed, attended, term, after, sems,
):
    copies = copies_of(
        [
            (qkv_hbm.at[:, D : 2 * D], key),
            (qkv_hbm.at[:, 2 * D : 3 * D], value),
            (out_hbm, out_weight),
            (final_hbm, final_weight),
        ],
        sems,
    )
    after[...] = arrived_ref[...].reshape(TPF, D)
    fill_picker(picker)
    parity = (iota((TPF, TPF), 0) ^ iota((TPF, TPF), 1)) & 1
    same[...] = jnp.where(parity == 0, 1.0, 0.0).astype(bf16)
    shift, scale = table[0:1, 0:D], 1.0 + table[0:1, D : 2 * D]
    gate = table[0:1, 2 * D : 3 * D]

    def modulate(rows):
        normed[rows, :] = (centre(after[rows, :].astype(f32)) * scale + shift).astype(bf16)

    by_rows(modulate)

    def ready(part):
        if part:
            copies[part - 1].wait()

    project(normed, (query, key, value), picker, raw, packed, ready)
    attend(packed, attended, same)
    copies[2].wait()
    copies[3].wait()
    for low, width in OUT_CHUNKS:
        term[:, low : low + width] = jnp.dot(
            attended[...], out_weight[:, low : low + width], preferred_element_type=f32
        ).astype(bf16)

    def finish(rows):
        state = after[rows, :].astype(f32) + gate * term[rows, :].astype(f32)
        normed[rows, :] = centre(state).astype(bf16)

    by_rows(finish)
    velocity_ref[:, 0:C] = lax.dot_general(
        normed[...], final_weight[...], (((1,), (1,)), ((), ())), preferred_element_type=f32
    )
    velocity_ref[:, C:] = jnp.zeros((TPF, LANES - C), f32)


def density_kernel(terms_ref, velocity_ref, now_ref, next_ref, log_ref, mean_ref):
    velocity = velocity_ref[...].T[0:C, :]
    factor, rest, spread, minus_log = (terms_ref[8 * row : 8 * row + 1, 0:1] for row in range(4))
    now = now_ref[0]
    drift = velocity + factor * (now + rest * velocity)
    next_mean = now - drift / STEPS
    standard = (next_ref[0] - next_mean) / spread
    log_ref[...] = (
        -0.5 * jnp.mean(standard * standard, 0, keepdims=True)
        + minus_log
        - 0.5 * math.log(2.0 * math.pi)
    )
    mean_ref[0] = next_mean


SMEM = pl.BlockSpec(memory_space=pltpu.SMEM)
HBM = pl.BlockSpec(memory_space=pltpu.HBM)
VMEM = pl.BlockSpec(memory_space=pltpu.VMEM)
work = [
    pltpu.VMEM((TPF, D), bf16),
    pltpu.VMEM((TPF, 2 * D), f32),
    pltpu.VMEM((TPF, 3 * D), bf16),
    pltpu.VMEM((TPF, D), bf16),
]


def in_hbm(array):
    return pltpu.with_memory_space_constraint(array, pltpu.HBM)


def shards(
    hidden,
    latents_now,
    latents_next,
    timestep,
    version_tags,
    noise_levels,
    time_weight,
    spatial_qkv,
    spatial_out,
    temporal_qkv,
    temporal_out,
    final_weight,
):
    time_weight, temporal_qkv = in_hbm(time_weight), in_hbm(temporal_qkv)
    part = pltpu.VMEM((D, D), bf16)
    picker = pltpu.VMEM((2 * D, LANES), bf16)
    after_spatial = pl.pallas_call(
        spatial_kernel,
        out_shape=jax.ShapeDtypeStruct((TPF // 2, 2, D), bf16),
        in_specs=[SMEM] + [HBM] * 4,
        out_specs=VMEM,
        scratch_shapes=[
            pltpu.VMEM((TPF, D), bf16),
            pltpu.VMEM((FREQ, 2 * D), bf16),
            pltpu.VMEM((FREQ, D), bf16),
            part,
            part,
            part,
            part,
            picker,
            *work,
            pltpu.SemaphoreType.DMA((7,)),
        ],
        compiler_params=pltpu.CompilerParams(vmem_limit_bytes=40 << 20),
        cost_estimate=pl.CostEstimate(
            flops=4 << 30, bytes_accessed=14 << 20, transcendentals=1 << 20
        ),
        name="spatial",
    )(timestep, in_hbm(hidden), time_weight, in_hbm(spatial_qkv), in_hbm(spatial_out))
    arrived = lax.all_to_all(
        after_spatial, ("inner", "outer"), split_axis=0, concat_axis=0, tiled=True
    )
    table, query, terms = pl.pallas_call(
        prepare_kernel,
        out_shape=(
            jax.ShapeDtypeStruct((8, 3 * D), f32),
            jax.ShapeDtypeStruct((D, D), bf16),
            jax.ShapeDtypeStruct((32, LANES), f32),
        ),
        in_specs=[SMEM] * 3 + [HBM] * 2,
        out_specs=(HBM, HBM, HBM),
        scratch_shapes=[
            pltpu.VMEM((FREQ, 3 * D), bf16),
            pltpu.VMEM((8, 3 * D), f32),
            pltpu.VMEM((32, LANES), f32),
            pltpu.SemaphoreType.DMA((4,)),
        ],
        compiler_params=pltpu.CompilerParams(vmem_limit_bytes=8 << 20),
        cost_estimate=pl.CostEstimate(
            flops=32 << 20, bytes_accessed=8 << 20, transcendentals=1 << 13
        ),
        name="prepare",
    )(timestep, version_tags, noise_levels, time_weight, temporal_qkv)
    velocity = pl.pallas_call(
        temporal_kernel,
        out_shape=jax.ShapeDtypeStruct((TPF, LANES), f32),
        in_specs=[VMEM] * 3 + [HBM] * 3,
        out_specs=VMEM,
        scratch_shapes=[
            picker,
            pltpu.VMEM((TPF, TPF), bf16),
            part,
            part,
            part,
            pltpu.VMEM((C, D), bf16),
            *work,
            pltpu.VMEM((TPF, D), bf16),
            pltpu.VMEM((TPF, D), bf16),
            pltpu.SemaphoreType.DMA((4,)),
        ],
        compiler_params=pltpu.CompilerParams(vmem_limit_bytes=40 << 20),
        cost_estimate=pl.CostEstimate(
            flops=4 << 30, bytes_accessed=12 << 20, transcendentals=1 << 20
        ),
        name="temporal",
    )(arrived, table, query, temporal_qkv, in_hbm(temporal_out), in_hbm(final_weight))
    returned = lax.all_to_all(
        velocity.reshape(TPF // 2, 2, LANES),
        ("inner", "outer"),
        split_axis=0,
        concat_axis=0,
        tiled=True,
    )
    return pl.pallas_call(
        density_kernel,
        out_shape=(
            jax.ShapeDtypeStruct((1, TPF), f32),
            jax.ShapeDtypeStruct((1, C, TPF), f32),
        ),
        in_specs=[VMEM] * 4,
        out_specs=(VMEM, VMEM),
        compiler_params=pltpu.CompilerParams(vmem_limit_bytes=4 << 20),
        name="density",
    )(terms, returned.reshape(TPF, LANES), latents_now, latents_next)


def solution(mesh):
    return jax.shard_map(
        shards,
        mesh=mesh,
        in_specs=(
            P(("inner", "outer"), None),
            P(("inner", "outer"), None, None),
            P(("inner", "outer"), None, None),
            P(),
            P(("inner", "outer")),
            P(),
            P(),
            P(),
            P(),
            P(),
            P(),
            P(),
        ),
        out_specs=(P(("inner", "outer"), None), P(("inner", "outer"), None, None)),
        check_vma=False,
    )
```

time: 63 us -> 59.4 us (0.943)
  blocking collectives: 0 us -> 14.6 us
  waiting for transfers between devices: 21.1 us -> 10.6 us
  starting transfers between devices: 16.4 us -> 11.5 us
  Pallas kernels: 23.3 us -> 20.5 us
    all_to_all x0 -> x1, blocking collectives: none -> 14.6 us  [shards(): lax.all_to_all(velocity.reshape(TPF // 2, 2, LANES), ('inner', 'outer'),...]
    all_to_all x1 -> x0, waiting for transfers between devices: 9.25 us -> none  [shards(): lax.all_to_all(velocity.reshape(TPF // 2, 2, LANES), ('inner', 'outer'),...]
    all_to_all x1 -> x0, starting transfers between devices: 4.86 us -> none  [shards(): lax.all_to_all(velocity.reshape(TPF // 2, 2, LANES), ('inner', 'outer'),...]
    pallas_call x1, Pallas kernels: 10 us -> 7.63 us  [shards(): pl.pallas_call(temporal_kernel, out_shape=jax.ShapeDtypeStruct((TPF, LANE...]
    all_to_all x1, waiting for transfers between devices: 11.8 us -> 10.6 us  [shards(): lax.all_to_all(after_spatial, ('inner', 'outer'), split_axis=0, concat_ax...]
  transfers between devices with their start and end apart: 2 -> 1, of which waited for: 2 -> 1; matrix products, arithmetic and copies ran while one was open for 0% -> 0% of each run, Pallas kernels for 4% -> 5%
where the time goes in v3:
time: 59.4 us; the launch traced here: 59.2 us
  Pallas kernels  20.5 us (35%)
  blocking collectives  14.6 us (25%)
  starting transfers between devices  11.5 us (19%)
  waiting for transfers between devices  10.6 us (18%)
  between operations  1.97 us (3%)
    all_to_all x1, blocking collectives, shards(): lax.all_to_all(velocity.reshape(TPF // 2, 2, LANES), ('inner', 'outer'),...  14.6 us
    all_to_all x1, starting transfers between devices, shards(): lax.all_to_all(after_spatial, ('inner', 'outer'), split_axis=0, concat_ax...  11.5 us
    all_to_all x1, waiting for transfers between devices, shards(): lax.all_to_all(after_spatial, ('inner', 'outer'), split_axis=0, concat_ax...  10.6 us
    pallas_call x1, Pallas kernels, shards(): pl.pallas_call(spatial_kernel, out_shape=jax.ShapeDtypeStruct((TPF // 2,...  9.32 us
    pallas_call x1, Pallas kernels, shards(): pl.pallas_call(temporal_kernel, out_shape=jax.ShapeDtypeStruct((TPF, LANE...  7.63 us
    pallas_call x1, Pallas kernels, shards(): pl.pallas_call(prepare_kernel, out_shape=(jax.ShapeDtypeStruct((8, 3 * D)...  2.86 us
  transfers between devices with their start and end apart: 1, of which 1 were waited for; matrix products, arithmetic and copies ran while one was open for 0% of the time, Pallas kernels for 5%

profile of v3, /device:TPU:1, one launch (start us, length us, event | category | flops | bytes accessed | tf_op | source)
XLA Modules:
  0.0 59.2 jit_solution(5351052383813986134)
XLA Ops:
  1.3 0.0 copy-start.2
  1.3 9.3 %spatial.1 = bf16[128,2,1152]{2,1,0:T(2,128)(2,1)} custom-call(s32[1]{0:T(128)S(6)} %copy.14.step_ref, bf16[256,1152]{1,0:T(8,128)(2,1)} %hidden_hbm.1, bf16[256,6912]{1,0:T(8,128)(2,1)} %time_hbm.3, bf16[1152,3456]{1,0:T(8,128)(2,1)} %qkv_hbm.4, bf16[1152,1152]{1,0:T(8,128)(2,1)} %out_hbm.2), custom_call_target="tpu_custom_call" | custom-call | flops 4294967296 | bytes 14680064 | tf_op jit(solution)/shard_map/spatial/pallas_call | solution.py:321
  10.6 11.5 %all-to-all-start = ((bf16[128,2,1152]{2,1,0:T(2,128)(2,1)}), bf16[128,2,1152]{2,1,0:T(2,128)(2,1)S(1)}, u32[]{:S(2)}, u32[]{:S(2)}) async-start(bf16[128,2,1152]{2,1,0:T(2,128)(2,1)} %spatial.1), calls=%async_computation | async-start | bytes 1179648 | tf_op jit(solution)/shard_map/all_to_all | solution.py:344
  22.8 0.0 copy-done.2
  22.8 2.9 %prepare.1 = (f32[8,3456]{1,0:T(8,128)S(1)}, bf16[1152,1152]{1,0:T(8,128)(2,1)S(1)}, f32[32,128]{1,0:T(8,128)S(1)}) custom-call(s32[1]{0:T(128)S(6)} %copy.14.step_ref, s32[1]{0:T(128)S(6)} %copy.15.tag_ref, f32[8]{0:T(128)S(1)} %copy-done.2, bf16[256,6912]{1,0:T(8,128)(2,1)} %time_hbm.3, bf16[1152,3456]{1,0:T(8,128)(2,1)} %qkv_hbm.5), custom_call_target="tpu_custom_call" | custom-call | flops 33554432 | bytes 8388608 | tf_op jit(solution)/shard_map/prepare/pallas_call | solution.py:347
  25.7 10.6 %all-to-all-done.arrived_ref = bf16[128,2,1152]{2,1,0:T(2,128)(2,1)S(1)} async-done(((bf16[128,2,1152]{2,1,0:T(2,128)(2,1)}), bf16[128,2,1152]{2,1,0:T(2,128)(2,1)S(1)}, u32[]{:S(2)}, u32[]{:S(2)}) %all-to-all-start) | async-done | bytes 589856 | tf_op jit(solution)/shard_map/all_to_all | solution.py:344
  36.2 0.0 copy-start
  36.2 0.0 copy-start.1
  36.2 7.6 %temporal.1 = f32[256,128]{1,0:T(8,128)S(1)} custom-call(bf16[128,2,1152]{2,1,0:T(2,128)(2,1)S(1)} %all-to-all-done.arrived_ref, f32[8,3456]{1,0:T(8,128)S(1)} %get-tuple-element.6.table, bf16[1152,1152]{1,0:T(8,128)(2,1)S(1)} %get-tuple-element.7.query, bf16[1152,3456]{1,0:T(8,128)(2,1)} %qkv_hbm.5, bf16[1152,1152]{1,0:T(8,128)(2,1)} %out_hbm.3, ...), custom_call_target="tpu_custom_call" | custom-call | flops 4294967296 | bytes 12582912 | tf_op jit(solution)/shard_map/temporal/pallas_call | solution.py:368
  43.9 14.6 %all_to_all.10 = f32[128,2,128]{2,1,0:T(2,128)S(1)} all-to-all(f32[128,2,128]{2,1,0:T(2,128)S(1)} %bitcast.3), channel_id=1, replica_groups=mesh['inner'=32,'outer'=4] {'inner','outer'}, dimensions={0} | all-to-all | bytes 262144 | tf_op jit(solution)/shard_map/all_to_all | solution.py:391
  58.5 0.0 copy-done
  58.5 0.0 copy-done.1
  58.5 0.7 %density.1 = (f32[1,256]{1,0:T(1,128)}, f32[1,16,256]{2,1,0:T(8,128)}) custom-call(f32[32,128]{1,0:T(8,128)S(1)} %get-tuple-element.5.terms_ref, f32[256,128]{1,0:T(8,128)S(1)} %bitcast.2, f32[1,16,256]{2,1,0:T(8,128)S(1)} %copy-done, f32[1,16,256]{2,1,0:T(8,128)S(1)} %copy-done.1), custom_call_target="tpu_custom_call" | custom-call | tf_op jit(solution)/shard_map/density/pallas_call | solution.py:398
Async XLA Ops:
  1.3 21.5 %copy-start.2 = (f32[8]{0:T(128)S(1)}, f32[8]{0:T(128)}, u32[]{:S(2)}) copy-start(f32[8]{0:T(128)} %level_ref.1) | copy-start | bytes 100
  10.6 25.6 %all-to-all-start = ((bf16[128,2,1152]{2,1,0:T(2,128)(2,1)}), bf16[128,2,1152]{2,1,0:T(2,128)(2,1)S(1)}, u32[]{:S(2)}, u32[]{:S(2)}) async-start(bf16[128,2,1152]{2,1,0:T(2,128)(2,1)} %spatial.1), calls=%async_computation | async-start | bytes 1179648 | tf_op jit(solution)/shard_map/all_to_all | solution.py:344
  36.2 22.3 %copy-start = (f32[1,16,256]{2,1,0:T(8,128)S(1)}, f32[1,16,256]{2,1,0:T(8,128)}, u32[]{:S(2)}) copy-start(f32[1,16,256]{2,1,0:T(8,128)} %now_ref.1) | copy-start | bytes 49156
  36.2 22.3 %copy-start.1 = (f32[1,16,256]{2,1,0:T(8,128)S(1)}, f32[1,16,256]{2,1,0:T(8,128)}, u32[]{:S(2)}) copy-start(f32[1,16,256]{2,1,0:T(8,128)} %next_ref.1) | copy-start | bytes 49156

commit v4 on v3

--- a/solution.py
+++ b/solution.py
@@ -17,6 +17,7 @@
 TPF = 256
 LANES = 128
 OUT_CHUNKS = tuple((low, min(512, D - low)) for low in range(0, D, 512))
+FIRST = 512
 ROWS = 32
 
 norm_eps = 1e-06
@@ -70,10 +71,9 @@
     return copies
 
 
-def project(normed, weights, picker, raw, packed, ready):
-    def product(part):
-        ready(part)
-        return jnp.dot(normed[...], weights[part][...], preferred_element_type=f32)
+def project(normed, weights, picker, raw, packed, ready, first):
+    def product(part, low=0, high=D):
+        return jnp.dot(normed[...], weights[part][:, low:high], preferred_element_type=f32)
 
     def square_sums(part):
         total = jnp.zeros((TPF, LANES), f32)
@@ -85,9 +85,15 @@
             )
         return total
 
-    raw[:, 0:D] = product(0)
+    ready(0)
+    raw[:, 0:first] = product(0, 0, first)
+    ready(1)
+    if first < D:
+        raw[:, first:D] = product(0, first, D)
+    ready(2)
     raw[:, D : 2 * D] = product(1)
     squares = square_sums(0)
+    ready(3)
     packed[:, 2 * D : 3 * D] = product(2).astype(bf16)
     squares = squares + square_sums(1)
     lane = iota((TPF, LANES), 1)
@@ -147,13 +153,15 @@
 
 def spatial_kernel(
     step_ref, hidden_hbm, time_hbm, qkv_hbm, out_hbm,
-    after_ref,
-    hidden, modulation, gate_weight, query, key, value, out_weight, picker, normed, raw,
+    after_hbm,
+    after_ref, hidden, modulation, gate_weight, query, key, value, out_weight, picker, normed, raw,
     packed, attended, sems,
 ):
     parts = (query, key, value)
     pairs = [(hidden_hbm, hidden), (time_hbm.at[:, 0 : 2 * D], modulation)]
-    pairs += [(qkv_hbm.at[:, part * D : (part + 1) * D], parts[part]) for part in range(3)]
+    for low, high in ((0, FIRST), (FIRST, D)):
+        pairs.append((qkv_hbm.at[:, low:high], query.at[:, low:high]))
+    pairs += [(qkv_hbm.at[:, part * D : (part + 1) * D], parts[part]) for part in (1, 2)]
     pairs += [(time_hbm.at[:, 2 * D : 3 * D], gate_weight), (out_hbm, out_weight)]
     copies = copies_of(pairs, sems)
 
@@ -173,17 +181,27 @@
         normed[rows, :] = (raw[rows, 0:D] * scale + shift).astype(bf16)
 
     by_rows(modulate)
-    project(normed, parts, picker, raw, packed, lambda part: copies[2 + part].wait())
+    project(normed, parts, picker, raw, packed, lambda piece: copies[2 + piece].wait(), FIRST)
     attend(packed, attended, None)
-    copies[5].wait()
     copies[6].wait()
+    copies[7].wait()
     gate = jnp.dot(activated, gate_weight[...], preferred_element_type=f32)[0:1, :]
+    sent = []
     for low, width in OUT_CHUNKS:
         projected = jnp.dot(
             attended[...], out_weight[:, low : low + width], preferred_element_type=f32
         )
         after = hidden[:, low : low + width].astype(f32) + gate[:, low : low + width] * projected
-        after_ref[:, :, low : low + width] = after.astype(bf16).reshape(TPF // 2, 2, width)
+        span = slice(low, low + width)
+        after_ref[:, :, span] = after.astype(bf16).reshape(TPF // 2, 2, width)
+        sent.append(
+            pltpu.make_async_copy(
+                after_ref.at[:, :, span], after_hbm.at[:, :, span], sems.at[8 + len(sent)]
+            )
+        )
+        sent[-1].start()
+    for copy in sent:
+        copy.wait()
 
 
 def prepare_kernel(
@@ -247,11 +265,11 @@
 
     by_rows(modulate)
 
-    def ready(part):
-        if part:
-            copies[part - 1].wait()
-
-    project(normed, (query, key, value), picker, raw, packed, ready)
+    def ready(piece):
+        if piece >= 2:
+            copies[piece - 2].wait()
+
+    project(normed, (query, key, value), picker, raw, packed, ready, D)
     attend(packed, attended, same)
     copies[2].wait()
     copies[3].wait()
@@ -322,8 +340,9 @@
         spatial_kernel,
         out_shape=jax.ShapeDtypeStruct((TPF // 2, 2, D), bf16),
         in_specs=[SMEM] + [HBM] * 4,
-        out_specs=VMEM,
+        out_specs=HBM,
         scratch_shapes=[
+            pltpu.VMEM((TPF // 2, 2, D), bf16),
             pltpu.VMEM((TPF, D), bf16),
             pltpu.VMEM((FREQ, 2 * D), bf16),
             pltpu.VMEM((FREQ, D), bf16),
@@ -333,7 +352,7 @@
             part,
             picker,
             *work,
-            pltpu.SemaphoreType.DMA((7,)),
+            pltpu.SemaphoreType.DMA((8 + len(OUT_CHUNKS),)),
         ],
         compiler_params=pltpu.CompilerParams(vmem_limit_bytes=40 << 20),
         cost_estimate=pl.CostEstimate(

time: 59.4 us -> 59.1 us (level)
  no operation moved by 1% of the time
where the time goes in v4:
time: 59.1 us; the launch traced here: 58.9 us
  Pallas kernels  20.2 us (34%)
  blocking collectives  14.6 us (25%)
  starting transfers between devices  11.5 us (19%)
  waiting for transfers between devices  10.6 us (18%)
  between operations  1.97 us (3%)
    all_to_all x1, blocking collectives, shards(): lax.all_to_all(velocity.reshape(TPF // 2, 2, LANES), ('inner', 'outer'),...  14.6 us
    all_to_all x1, starting transfers between devices, shards(): lax.all_to_all(after_spatial, ('inner', 'outer'), split_axis=0, concat_ax...  11.5 us
    all_to_all x1, waiting for transfers between devices, shards(): lax.all_to_all(after_spatial, ('inner', 'outer'), split_axis=0, concat_ax...  10.6 us
    pallas_call x1, Pallas kernels, shards(): pl.pallas_call(spatial_kernel, out_shape=jax.ShapeDtypeStruct((TPF // 2,...  8.97 us
    pallas_call x1, Pallas kernels, shards(): pl.pallas_call(temporal_kernel, out_shape=jax.ShapeDtypeStruct((TPF, LANE...  7.63 us
    pallas_call x1, Pallas kernels, shards(): pl.pallas_call(prepare_kernel, out_shape=(jax.ShapeDtypeStruct((8, 3 * D)...  2.86 us
  transfers between devices with their start and end apart: 1, of which 1 were waited for; matrix products, arithmetic and copies ran while one was open for 0% of the time, Pallas kernels for 5%

profile of v4, /device:TPU:1, one launch (start us, length us, event | category | flops | bytes accessed | tf_op | source)
XLA Modules:
  0.0 58.9 jit_solution(803158087150965518)
XLA Ops:
  1.3 0.0 copy-start.2
  1.3 9.0 %spatial.1 = bf16[128,2,1152]{2,1,0:T(2,128)(2,1)} custom-call(s32[1]{0:T(128)S(6)} %copy.14.step_ref, bf16[256,1152]{1,0:T(8,128)(2,1)} %hidden_hbm.1, bf16[256,6912]{1,0:T(8,128)(2,1)} %time_hbm.3, bf16[1152,3456]{1,0:T(8,128)(2,1)} %qkv_hbm.4, bf16[1152,1152]{1,0:T(8,128)(2,1)} %out_hbm.2), custom_call_target="tpu_custom_call" | custom-call | flops 4294967296 | bytes 14680064 | tf_op jit(solution)/shard_map/spatial/pallas_call | solution.py:339
  10.3 11.5 %all-to-all-start = ((bf16[128,2,1152]{2,1,0:T(2,128)(2,1)}), bf16[128,2,1152]{2,1,0:T(2,128)(2,1)S(1)}, u32[]{:S(2)}, u32[]{:S(2)}) async-start(bf16[128,2,1152]{2,1,0:T(2,128)(2,1)} %spatial.1), calls=%async_computation | async-start | bytes 1179648 | tf_op jit(solution)/shard_map/all_to_all | solution.py:363
  22.4 0.0 copy-done.2
  22.4 2.9 %prepare.1 = (f32[8,3456]{1,0:T(8,128)S(1)}, bf16[1152,1152]{1,0:T(8,128)(2,1)S(1)}, f32[32,128]{1,0:T(8,128)S(1)}) custom-call(s32[1]{0:T(128)S(6)} %copy.14.step_ref, s32[1]{0:T(128)S(6)} %copy.15.tag_ref, f32[8]{0:T(128)S(1)} %copy-done.2, bf16[256,6912]{1,0:T(8,128)(2,1)} %time_hbm.3, bf16[1152,3456]{1,0:T(8,128)(2,1)} %qkv_hbm.5), custom_call_target="tpu_custom_call" | custom-call | flops 33554432 | bytes 8388608 | tf_op jit(solution)/shard_map/prepare/pallas_call | solution.py:366
  25.3 10.6 %all-to-all-done.arrived_ref = bf16[128,2,1152]{2,1,0:T(2,128)(2,1)S(1)} async-done(((bf16[128,2,1152]{2,1,0:T(2,128)(2,1)}), bf16[128,2,1152]{2,1,0:T(2,128)(2,1)S(1)}, u32[]{:S(2)}, u32[]{:S(2)}) %all-to-all-start) | async-done | bytes 589856 | tf_op jit(solution)/shard_map/all_to_all | solution.py:363
  35.9 0.0 copy-start
  35.9 0.0 copy-start.1
  35.9 7.6 %temporal.1 = f32[256,128]{1,0:T(8,128)S(1)} custom-call(bf16[128,2,1152]{2,1,0:T(2,128)(2,1)S(1)} %all-to-all-done.arrived_ref, f32[8,3456]{1,0:T(8,128)S(1)} %get-tuple-element.6.table, bf16[1152,1152]{1,0:T(8,128)(2,1)S(1)} %get-tuple-element.7.query, bf16[1152,3456]{1,0:T(8,128)(2,1)} %qkv_hbm.5, bf16[1152,1152]{1,0:T(8,128)(2,1)} %out_hbm.3, ...), custom_call_target="tpu_custom_call" | custom-call | flops 4294967296 | bytes 12582912 | tf_op jit(solution)/shard_map/temporal/pallas_call | solution.py:387
  43.5 14.6 %all_to_all.10 = f32[128,2,128]{2,1,0:T(2,128)S(1)} all-to-all(f32[128,2,128]{2,1,0:T(2,128)S(1)} %bitcast.3), channel_id=1, replica_groups=mesh['inner'=32,'outer'=4] {'inner','outer'}, dimensions={0} | all-to-all | bytes 262144 | tf_op jit(solution)/shard_map/all_to_all | solution.py:410
  58.2 0.0 copy-done
  58.2 0.0 copy-done.1
  58.2 0.7 %density.1 = (f32[1,256]{1,0:T(1,128)}, f32[1,16,256]{2,1,0:T(8,128)}) custom-call(f32[32,128]{1,0:T(8,128)S(1)} %get-tuple-element.5.terms_ref, f32[256,128]{1,0:T(8,128)S(1)} %bitcast.2, f32[1,16,256]{2,1,0:T(8,128)S(1)} %copy-done, f32[1,16,256]{2,1,0:T(8,128)S(1)} %copy-done.1), custom_call_target="tpu_custom_call" | custom-call | tf_op jit(solution)/shard_map/density/pallas_call | solution.py:417
Async XLA Ops:
  1.3 21.2 %copy-start.2 = (f32[8]{0:T(128)S(1)}, f32[8]{0:T(128)}, u32[]{:S(2)}) copy-start(f32[8]{0:T(128)} %level_ref.1) | copy-start | bytes 100
  10.3 25.6 %all-to-all-start = ((bf16[128,2,1152]{2,1,0:T(2,128)(2,1)}), bf16[128,2,1152]{2,1,0:T(2,128)(2,1)S(1)}, u32[]{:S(2)}, u32[]{:S(2)}) async-start(bf16[128,2,1152]{2,1,0:T(2,128)(2,1)} %spatial.1), calls=%async_computation | async-start | bytes 1179648 | tf_op jit(solution)/shard_map/all_to_all | solution.py:363
  35.9 22.3 %copy-start = (f32[1,16,256]{2,1,0:T(8,128)S(1)}, f32[1,16,256]{2,1,0:T(8,128)}, u32[]{:S(2)}) copy-start(f32[1,16,256]{2,1,0:T(8,128)} %now_ref.1) | copy-start | bytes 49156
  35.9 22.3 %copy-start.1 = (f32[1,16,256]{2,1,0:T(8,128)S(1)}, f32[1,16,256]{2,1,0:T(8,128)}, u32[]{:S(2)}) copy-start(f32[1,16,256]{2,1,0:T(8,128)} %next_ref.1) | copy-start | bytes 49156

commit v5 on v4

--- a/solution.py
+++ b/solution.py
@@ -17,7 +17,8 @@
 TPF = 256
 LANES = 128
 OUT_CHUNKS = tuple((low, min(512, D - low)) for low in range(0, D, 512))
-FIRST = 512
+CUTS = (0, 512, 1280, 2 * D, 3 * D)
+EARLY = 1024
 ROWS = 32
 
 norm_eps = 1e-06
@@ -37,11 +38,8 @@
 
 def fill_picker(picker):
     for low in range(0, 2 * D, 256):
-        column = iota((256, LANES), 0) + low
-        lane = iota((256, LANES), 1)
-        head = jnp.where(lane < 2 * HEADS, lane, lane - 2 * HEADS)
-        offset = column - head * HEAD
-        inside = (offset >= 0) & (offset < HEAD) & (lane < 4 * HEADS)
+        offset = iota((256, LANES), 0) + low - iota((256, LANES), 1) * HEAD
+        inside = (offset >= 0) & (offset < HEAD)
         picker[low : low + 256, :] = jnp.where(inside, 1.0, 0.0).astype(bf16)
 
 
@@ -71,49 +69,28 @@
     return copies
 
 
-def project(normed, weights, picker, raw, packed, ready, first):
-    def product(part, low=0, high=D):
-        return jnp.dot(normed[...], weights[part][:, low:high], preferred_element_type=f32)
-
-    def square_sums(part):
-        total = jnp.zeros((TPF, LANES), f32)
-        for low, width in OUT_CHUNKS:
-            span = slice(part * D + low, part * D + low + width)
-            values = raw[:, span]
-            total = total + jnp.dot(
-                (values * values).astype(bf16), picker[span, :], preferred_element_type=f32
-            )
-        return total
-
-    ready(0)
-    raw[:, 0:first] = product(0, 0, first)
-    ready(1)
-    if first < D:
-        raw[:, first:D] = product(0, first, D)
-    ready(2)
-    raw[:, D : 2 * D] = product(1)
-    squares = square_sums(0)
-    ready(3)
-    packed[:, 2 * D : 3 * D] = product(2).astype(bf16)
-    squares = squares + square_sums(1)
+def project(normed, pieces, picker, packed):
+    squares = jnp.zeros((TPF, LANES), f32)
+    before = None
+    for low, high, weight, wait in pieces:
+        wait()
+        mixed = jnp.dot(normed[...], weight[...], preferred_element_type=f32)
+        packed[:, low:high] = mixed.astype(bf16)
+        if before:
+            for left in range(before[0], before[1], 512):
+                span = slice(left, min(left + 512, before[1]))
+                values = packed[:, span].astype(f32)
+                squares = squares + jnp.dot(
+                    (values * values).astype(bf16), picker[span, :], preferred_element_type=f32
+                )
+        before = (low, high)
+    factor = lax.rsqrt(squares * (1.0 / HEAD) + norm_eps)
     lane = iota((TPF, LANES), 1)
-    head = jnp.where(lane < 2 * HEADS, lane, lane - 2 * HEADS)
-    factor = lax.rsqrt(squares * (1.0 / HEAD) + norm_eps)
-    factor = factor * jnp.where(head < HEADS, HEAD ** (-0.5) * math.log2(math.e), 1.0)
-    coarse = factor.astype(bf16)
-    fine = (factor - coarse.astype(f32)).astype(bf16)
-    both = jnp.where(lane < 2 * HEADS, coarse.astype(f32), fine.astype(f32)).astype(bf16)
-    for low in range(0, 2 * D, 256):
-        spread = lax.dot_general(
-            both,
-            picker[low : low + 256, :],
-            (((1,), (1,)), ((), ())),
-            preferred_element_type=f32,
-        )
-        packed[:, low : low + 256] = (raw[:, low : low + 256] * spread).astype(bf16)
-
-
-def attend(packed, attended, same):
+    return factor * jnp.where(lane < HEADS, HEAD ** (-0.5) * math.log2(math.e), 1.0)
+
+
+def attend(packed, factor, attended, same):
+    across = factor.T
     ones = jnp.ones((TPF, LANES), bf16)
     lane = iota((TPF, LANES), 1)
     pending = None
@@ -130,6 +107,8 @@
             (((1,), (1,)), ((), ())),
             preferred_element_type=f32,
         )
+        scores = scores * factor[:, head : head + 1]
+        scores = scores * across[HEADS + head : HEADS + head + 1, :]
         weights = jnp.exp2(scores).astype(bf16)
         if same is not None:
             weights = weights * same[...]
@@ -154,14 +133,13 @@
 def spatial_kernel(
     step_ref, hidden_hbm, time_hbm, qkv_hbm, out_hbm,
     after_hbm,
-    after_ref, hidden, modulation, gate_weight, query, key, value, out_weight, picker, normed, raw,
-    packed, attended, sems,
+    after_ref, hidden, modulation, gate_weight, out_weight, picker, raw, normed, packed, attended,
+    sems, *parts,
 ):
-    parts = (query, key, value)
     pairs = [(hidden_hbm, hidden), (time_hbm.at[:, 0 : 2 * D], modulation)]
-    for low, high in ((0, FIRST), (FIRST, D)):
-        pairs.append((qkv_hbm.at[:, low:high], query.at[:, low:high]))
-    pairs += [(qkv_hbm.at[:, part * D : (part + 1) * D], parts[part]) for part in (1, 2)]
+    pairs += [
+        (qkv_hbm.at[:, low:high], part) for low, high, part in zip(CUTS, CUTS[1:], parts)
+    ]
     pairs += [(time_hbm.at[:, 2 * D : 3 * D], gate_weight), (out_hbm, out_weight)]
     copies = copies_of(pairs, sems)
 
@@ -181,8 +159,9 @@
         normed[rows, :] = (raw[rows, 0:D] * scale + shift).astype(bf16)
 
     by_rows(modulate)
-    project(normed, parts, picker, raw, packed, lambda piece: copies[2 + piece].wait(), FIRST)
-    attend(packed, attended, None)
+    waits = [copy.wait for copy in copies[2:6]]
+    factor = project(normed, list(zip(CUTS, CUTS[1:], parts, waits)), picker, packed)
+    attend(packed, factor, attended, None)
     copies[6].wait()
     copies[7].wait()
     gate = jnp.dot(activated, gate_weight[...], preferred_element_type=f32)[0:1, :]
@@ -206,13 +185,13 @@
 
 def prepare_kernel(
     step_ref, tag_ref, level_ref, time_hbm, qkv_hbm,
-    table_hbm, query_hbm, terms_hbm,
+    table_hbm, early_hbm, terms_hbm,
     modulation, table, terms, sems,
 ):
     copies = copies_of(
         [
             (time_hbm.at[:, 3 * D : 6 * D], modulation),
-            (qkv_hbm.at[:, 0:D], query_hbm),
+            (qkv_hbm.at[:, 0:EARLY], early_hbm),
         ],
         sems,
     )
@@ -239,14 +218,14 @@
 
 
 def temporal_kernel(
-    arrived_ref, table, query, qkv_hbm, out_hbm, final_hbm,
+    arrived_ref, table, early, qkv_hbm, out_hbm, final_hbm,
     velocity_ref,
-    picker, same, key, value, out_weight, final_weight,
-    normed, raw, packed, attended, term, after, sems,
+    picker, same, middle, value, out_weight, final_weight,
+    normed, packed, attended, term, after, sems,
 ):
     copies = copies_of(
         [
-            (qkv_hbm.at[:, D : 2 * D], key),
+            (qkv_hbm.at[:, EARLY : 2 * D], middle),
             (qkv_hbm.at[:, 2 * D : 3 * D], value),
             (out_hbm, out_weight),
             (final_hbm, final_weight),
@@ -265,12 +244,13 @@
 
     by_rows(modulate)
 
-    def ready(piece):
-        if piece >= 2:
-            copies[piece - 2].wait()
-
-    project(normed, (query, key, value), picker, raw, packed, ready, D)
-    attend(packed, attended, same)
+    pieces = [
+        (0, EARLY, early, lambda: None),
+        (EARLY, 2 * D, middle, copies[0].wait),
+        (2 * D, 3 * D, value, copies[1].wait),
+    ]
+    factor = project(normed, pieces, picker, packed)
+    attend(packed, factor, attended, same)
     copies[2].wait()
     copies[3].wait()
     for low, width in OUT_CHUNKS:
@@ -309,7 +289,6 @@
 VMEM = pl.BlockSpec(memory_space=pltpu.VMEM)
 work = [
     pltpu.VMEM((TPF, D), bf16),
-    pltpu.VMEM((TPF, 2 * D), f32),
     pltpu.VMEM((TPF, 3 * D), bf16),
     pltpu.VMEM((TPF, D), bf16),
 ]
@@ -334,7 +313,6 @@
     final_weight,
 ):
     time_weight, temporal_qkv = in_hbm(time_weight), in_hbm(temporal_qkv)
-    part = pltpu.VMEM((D, D), bf16)
     picker = pltpu.VMEM((2 * D, LANES), bf16)
     after_spatial = pl.pallas_call(
         spatial_kernel,
@@ -346,13 +324,12 @@
             pltpu.VMEM((TPF, D), bf16),
             pltpu.VMEM((FREQ, 2 * D), bf16),
             pltpu.VMEM((FREQ, D), bf16),
-            part,
-            part,
-            part,
-            part,
+            pltpu.VMEM((D, D), bf16),
             picker,
+            pltpu.VMEM((TPF, D), f32),
             *work,
             pltpu.SemaphoreType.DMA((8 + len(OUT_CHUNKS),)),
+            *(pltpu.VMEM((D, high - low), bf16) for low, high in zip(CUTS, CUTS[1:])),
         ],
         compiler_params=pltpu.CompilerParams(vmem_limit_bytes=40 << 20),
         cost_estimate=pl.CostEstimate(
@@ -363,11 +340,11 @@
     arrived = lax.all_to_all(
         after_spatial, ("inner", "outer"), split_axis=0, concat_axis=0, tiled=True
     )
-    table, query, terms = pl.pallas_call(
+    table, early, terms = pl.pallas_call(
         prepare_kernel,
         out_shape=(
             jax.ShapeDtypeStruct((8, 3 * D), f32),
-            jax.ShapeDtypeStruct((D, D), bf16),
+            jax.ShapeDtypeStruct((D, EARLY), bf16),
             jax.ShapeDtypeStruct((32, LANES), f32),
         ),
         in_specs=[SMEM] * 3 + [HBM] * 2,
@@ -392,9 +369,9 @@
         scratch_shapes=[
             picker,
             pltpu.VMEM((TPF, TPF), bf16),
-            part,
-            part,
-            part,
+            pltpu.VMEM((D, 2 * D - EARLY), bf16),
+            pltpu.VMEM((D, D), bf16),
+            pltpu.VMEM((D, D), bf16),
             pltpu.VMEM((C, D), bf16),
             *work,
             pltpu.VMEM((TPF, D), bf16),
@@ -406,7 +383,7 @@
             flops=4 << 30, bytes_accessed=12 << 20, transcendentals=1 << 20
         ),
         name="temporal",
-    )(arrived, table, query, temporal_qkv, in_hbm(temporal_out), in_hbm(final_weight))
+    )(arrived, table, early, temporal_qkv, in_hbm(temporal_out), in_hbm(final_weight))
     returned = lax.all_to_all(
         velocity.reshape(TPF // 2, 2, LANES),
         ("inner", "outer"),

time: 59.1 us -> 58.8 us (level)
  no operation moved by 1% of the time
where the time goes in v5:
time: 58.8 us; the launch traced here: 58.6 us
  Pallas kernels  19.8 us (34%)
  blocking collectives  14.6 us (25%)
  starting transfers between devices  11.5 us (20%)
  waiting for transfers between devices  10.7 us (18%)
  between operations  1.97 us (3%)
    all_to_all x1, blocking collectives, shards(): lax.all_to_all(velocity.reshape(TPF // 2, 2, LANES), ('inner', 'outer'),...  14.6 us
    all_to_all x1, starting transfers between devices, shards(): lax.all_to_all(after_spatial, ('inner', 'outer'), split_axis=0, concat_ax...  11.5 us
    all_to_all x1, waiting for transfers between devices, shards(): lax.all_to_all(after_spatial, ('inner', 'outer'), split_axis=0, concat_ax...  10.7 us
    pallas_call x1, Pallas kernels, shards(): pl.pallas_call(spatial_kernel, out_shape=jax.ShapeDtypeStruct((TPF // 2,...  8.84 us
    pallas_call x1, Pallas kernels, shards(): pl.pallas_call(temporal_kernel, out_shape=jax.ShapeDtypeStruct((TPF, LANE...  7.46 us
    pallas_call x1, Pallas kernels, shards(): pl.pallas_call(prepare_kernel, out_shape=(jax.ShapeDtypeStruct((8, 3 * D)...  2.78 us
  transfers between devices with their start and end apart: 1, of which 1 were waited for; matrix products, arithmetic and copies ran while one was open for 0% of the time, Pallas kernels for 5%

profile of v5, /device:TPU:1, one launch (start us, length us, event | category | flops | bytes accessed | tf_op | source)
XLA Modules:
  0.0 58.6 jit_solution(12809352683162823977)
XLA Ops:
  1.3 0.0 copy-start.2
  1.3 8.8 %spatial.1 = bf16[128,2,1152]{2,1,0:T(2,128)(2,1)} custom-call(s32[1]{0:T(128)S(6)} %copy.14.step_ref, bf16[256,1152]{1,0:T(8,128)(2,1)} %hidden_hbm.1, bf16[256,6912]{1,0:T(8,128)(2,1)} %time_hbm.3, bf16[1152,3456]{1,0:T(8,128)(2,1)} %qkv_hbm.4, bf16[1152,1152]{1,0:T(8,128)(2,1)} %out_hbm.2), custom_call_target="tpu_custom_call" | custom-call | flops 4294967296 | bytes 14680064 | tf_op jit(solution)/shard_map/spatial/pallas_call | solution.py:317
  10.1 11.5 %all-to-all-start = ((bf16[128,2,1152]{2,1,0:T(2,128)(2,1)}), bf16[128,2,1152]{2,1,0:T(2,128)(2,1)S(1)}, u32[]{:S(2)}, u32[]{:S(2)}) async-start(bf16[128,2,1152]{2,1,0:T(2,128)(2,1)} %spatial.1), calls=%async_computation | async-start | bytes 1179648 | tf_op jit(solution)/shard_map/all_to_all | solution.py:340
  22.3 0.0 copy-done.2
  22.3 2.8 %prepare.1 = (f32[8,3456]{1,0:T(8,128)S(1)}, bf16[1152,1024]{1,0:T(8,128)(2,1)S(1)}, f32[32,128]{1,0:T(8,128)S(1)}) custom-call(s32[1]{0:T(128)S(6)} %copy.14.step_ref, s32[1]{0:T(128)S(6)} %copy.15.tag_ref, f32[8]{0:T(128)S(1)} %copy-done.2, bf16[256,6912]{1,0:T(8,128)(2,1)} %time_hbm.3, bf16[1152,3456]{1,0:T(8,128)(2,1)} %qkv_hbm.5), custom_call_target="tpu_custom_call" | custom-call | flops 33554432 | bytes 8388608 | tf_op jit(solution)/shard_map/prepare/pallas_call | solution.py:343
  25.1 10.7 %all-to-all-done.arrived_ref = bf16[128,2,1152]{2,1,0:T(2,128)(2,1)S(1)} async-done(((bf16[128,2,1152]{2,1,0:T(2,128)(2,1)}), bf16[128,2,1152]{2,1,0:T(2,128)(2,1)S(1)}, u32[]{:S(2)}, u32[]{:S(2)}) %all-to-all-start) | async-done | bytes 589856 | tf_op jit(solution)/shard_map/all_to_all | solution.py:340
  35.8 0.0 copy-start
  35.8 0.0 copy-start.1
  35.8 7.5 %temporal.1 = f32[256,128]{1,0:T(8,128)S(1)} custom-call(bf16[128,2,1152]{2,1,0:T(2,128)(2,1)S(1)} %all-to-all-done.arrived_ref, f32[8,3456]{1,0:T(8,128)S(1)} %get-tuple-element.6.table, bf16[1152,1024]{1,0:T(8,128)(2,1)S(1)} %get-tuple-element.7.early, bf16[1152,3456]{1,0:T(8,128)(2,1)} %qkv_hbm.5, bf16[1152,1152]{1,0:T(8,128)(2,1)} %out_hbm.3, ...), custom_call_target="tpu_custom_call" | custom-call | flops 4294967296 | bytes 12582912 | tf_op jit(solution)/shard_map/temporal/pallas_call | solution.py:364
  43.2 14.6 %all_to_all.10 = f32[128,2,128]{2,1,0:T(2,128)S(1)} all-to-all(f32[128,2,128]{2,1,0:T(2,128)S(1)} %bitcast.3), channel_id=1, replica_groups=mesh['inner'=32,'outer'=4] {'inner','outer'}, dimensions={0} | all-to-all | bytes 262144 | tf_op jit(solution)/shard_map/all_to_all | solution.py:387
  57.9 0.0 copy-done
  57.9 0.0 copy-done.1
  57.9 0.7 %density.1 = (f32[1,256]{1,0:T(1,128)}, f32[1,16,256]{2,1,0:T(8,128)}) custom-call(f32[32,128]{1,0:T(8,128)S(1)} %get-tuple-element.5.terms_ref, f32[256,128]{1,0:T(8,128)S(1)} %bitcast.2, f32[1,16,256]{2,1,0:T(8,128)S(1)} %copy-done, f32[1,16,256]{2,1,0:T(8,128)S(1)} %copy-done.1), custom_call_target="tpu_custom_call" | custom-call | tf_op jit(solution)/shard_map/density/pallas_call | solution.py:394
Async XLA Ops:
  1.3 21.0 %copy-start.2 = (f32[8]{0:T(128)S(1)}, f32[8]{0:T(128)}, u32[]{:S(2)}) copy-start(f32[8]{0:T(128)} %level_ref.1) | copy-start | bytes 100
  10.1 25.6 %all-to-all-start = ((bf16[128,2,1152]{2,1,0:T(2,128)(2,1)}), bf16[128,2,1152]{2,1,0:T(2,128)(2,1)S(1)}, u32[]{:S(2)}, u32[]{:S(2)}) async-start(bf16[128,2,1152]{2,1,0:T(2,128)(2,1)} %spatial.1), calls=%async_computation | async-start | bytes 1179648 | tf_op jit(solution)/shard_map/all_to_all | solution.py:340
  35.8 22.1 %copy-start = (f32[1,16,256]{2,1,0:T(8,128)S(1)}, f32[1,16,256]{2,1,0:T(8,128)}, u32[]{:S(2)}) copy-start(f32[1,16,256]{2,1,0:T(8,128)} %now_ref.1) | copy-start | bytes 49156
  35.8 22.1 %copy-start.1 = (f32[1,16,256]{2,1,0:T(8,128)S(1)}, f32[1,16,256]{2,1,0:T(8,128)}, u32[]{:S(2)}) copy-start(f32[1,16,256]{2,1,0:T(8,128)} %next_ref.1) | copy-start | bytes 49156

commit v6 on v5

--- a/solution.py
+++ b/solution.py
@@ -184,14 +184,15 @@
 
 
 def prepare_kernel(
-    step_ref, tag_ref, level_ref, time_hbm, qkv_hbm,
-    table_hbm, early_hbm, terms_hbm,
-    modulation, table, terms, sems,
+    step_ref, tag_ref, level_ref, time_hbm, qkv_hbm, final_hbm,
+    table_hbm, early_hbm, terms_hbm, head_hbm,
+    modulation, final_weight, table, terms, head_weight, sems,
 ):
     copies = copies_of(
         [
             (time_hbm.at[:, 3 * D : 6 * D], modulation),
             (qkv_hbm.at[:, 0:EARLY], early_hbm),
+            (final_hbm, final_weight),
         ],
         sems,
     )
@@ -206,9 +207,13 @@
     terms[24:32, :] = -jnp.log(spread)
     copies[0].wait()
     table[...] = jnp.dot(activated, modulation[...], preferred_element_type=f32)[0:8]
+    copies[2].wait()
+    padded = jnp.concatenate([final_weight[...].astype(f32), jnp.zeros((LANES - C, D), f32)], 0)
+    head_weight[...] = padded.T.astype(bf16)
     results = [
-        pltpu.make_async_copy(table, table_hbm, sems.at[2]),
-        pltpu.make_async_copy(terms, terms_hbm, sems.at[3]),
+        pltpu.make_async_copy(table, table_hbm, sems.at[3]),
+        pltpu.make_async_copy(terms, terms_hbm, sems.at[4]),
+        pltpu.make_async_copy(head_weight, head_hbm, sems.at[5]),
     ]
     for copy in results:
         copy.start()
@@ -218,9 +223,9 @@
 
 
 def temporal_kernel(
-    arrived_ref, table, early, qkv_hbm, out_hbm, final_hbm,
+    arrived_ref, table, early, head_weight, qkv_hbm, out_hbm,
     velocity_ref,
-    picker, same, middle, value, out_weight, final_weight,
+    picker, same, middle, value, out_weight,
     normed, packed, attended, term, after, sems,
 ):
     copies = copies_of(
@@ -228,7 +233,6 @@
             (qkv_hbm.at[:, EARLY : 2 * D], middle),
             (qkv_hbm.at[:, 2 * D : 3 * D], value),
             (out_hbm, out_weight),
-            (final_hbm, final_weight),
         ],
         sems,
     )
@@ -252,7 +256,6 @@
     factor = project(normed, pieces, picker, packed)
     attend(packed, factor, attended, same)
     copies[2].wait()
-    copies[3].wait()
     for low, width in OUT_CHUNKS:
         term[:, low : low + width] = jnp.dot(
             attended[...], out_weight[:, low : low + width], preferred_element_type=f32
@@ -263,10 +266,7 @@
         normed[rows, :] = centre(state).astype(bf16)
 
     by_rows(finish)
-    velocity_ref[:, 0:C] = lax.dot_general(
-        normed[...], final_weight[...], (((1,), (1,)), ((), ())), preferred_element_type=f32
-    )
-    velocity_ref[:, C:] = jnp.zeros((TPF, LANES - C), f32)
+    velocity_ref[...] = jnp.dot(normed[...], head_weight[...], preferred_element_type=f32)
 
 
 def density_kernel(terms_ref, velocity_ref, now_ref, next_ref, log_ref, mean_ref):
@@ -340,31 +340,34 @@
     arrived = lax.all_to_all(
         after_spatial, ("inner", "outer"), split_axis=0, concat_axis=0, tiled=True
     )
-    table, early, terms = pl.pallas_call(
+    table, early, terms, head_weight = pl.pallas_call(
         prepare_kernel,
         out_shape=(
             jax.ShapeDtypeStruct((8, 3 * D), f32),
             jax.ShapeDtypeStruct((D, EARLY), bf16),
             jax.ShapeDtypeStruct((32, LANES), f32),
-        ),
-        in_specs=[SMEM] * 3 + [HBM] * 2,
-        out_specs=(HBM, HBM, HBM),
+            jax.ShapeDtypeStruct((D, LANES), bf16),
+        ),
+        in_specs=[SMEM] * 3 + [HBM] * 3,
+        out_specs=(HBM, HBM, HBM, HBM),
         scratch_shapes=[
             pltpu.VMEM((FREQ, 3 * D), bf16),
+            pltpu.VMEM((C, D), bf16),
             pltpu.VMEM((8, 3 * D), f32),
             pltpu.VMEM((32, LANES), f32),
-            pltpu.SemaphoreType.DMA((4,)),
+            pltpu.VMEM((D, LANES), bf16),
+            pltpu.SemaphoreType.DMA((6,)),
         ],
         compiler_params=pltpu.CompilerParams(vmem_limit_bytes=8 << 20),
         cost_estimate=pl.CostEstimate(
             flops=32 << 20, bytes_accessed=8 << 20, transcendentals=1 << 13
         ),
         name="prepare",
-    )(timestep, version_tags, noise_levels, time_weight, temporal_qkv)
+    )(timestep, version_tags, noise_levels, time_weight, temporal_qkv, in_hbm(final_weight))
     velocity = pl.pallas_call(
         temporal_kernel,
         out_shape=jax.ShapeDtypeStruct((TPF, LANES), f32),
-        in_specs=[VMEM] * 3 + [HBM] * 3,
+        in_specs=[VMEM] * 4 + [HBM] * 2,
         out_specs=VMEM,
         scratch_shapes=[
             picker,
@@ -372,18 +375,17 @@
             pltpu.VMEM((D, 2 * D - EARLY), bf16),
             pltpu.VMEM((D, D), bf16),
             pltpu.VMEM((D, D), bf16),
-            pltpu.VMEM((C, D), bf16),
             *work,
             pltpu.VMEM((TPF, D), bf16),
             pltpu.VMEM((TPF, D), bf16),
-            pltpu.SemaphoreType.DMA((4,)),
+            pltpu.SemaphoreType.DMA((3,)),
         ],
         compiler_params=pltpu.CompilerParams(vmem_limit_bytes=40 << 20),
         cost_estimate=pl.CostEstimate(
             flops=4 << 30, bytes_accessed=12 << 20, transcendentals=1 << 20
         ),
         name="temporal",
-    )(arrived, table, early, temporal_qkv, in_hbm(temporal_out), in_hbm(final_weight))
+    )(arrived, table, early, head_weight, temporal_qkv, in_hbm(temporal_out))
     returned = lax.all_to_all(
         velocity.reshape(TPF // 2, 2, LANES),
         ("inner", "outer"),

time: 58.8 us -> 58.7 us (level)
  no operation moved by 1% of the time
where the time goes in v6:
time: 58.7 us; the launch traced here: 58.4 us
  Pallas kernels  19.9 us (34%)
  blocking collectives  14.6 us (25%)
  starting transfers between devices  11.5 us (20%)
  waiting for transfers between devices  10.4 us (18%)
  between operations  1.97 us (3%)
    all_to_all x1, blocking collectives, shards(): lax.all_to_all(velocity.reshape(TPF // 2, 2, LANES), ('inner', 'outer'),...  14.6 us
    all_to_all x1, starting transfers between devices, shards(): lax.all_to_all(after_spatial, ('inner', 'outer'), split_axis=0, concat_ax...  11.5 us
    all_to_all x1, waiting for transfers between devices, shards(): lax.all_to_all(after_spatial, ('inner', 'outer'), split_axis=0, concat_ax...  10.4 us
    pallas_call x1, Pallas kernels, shards(): pl.pallas_call(spatial_kernel, out_shape=jax.ShapeDtypeStruct((TPF // 2,...  8.84 us
    pallas_call x1, Pallas kernels, shards(): pl.pallas_call(temporal_kernel, out_shape=jax.ShapeDtypeStruct((TPF, LANE...  7.34 us
    pallas_call x1, Pallas kernels, shards(): pl.pallas_call(prepare_kernel, out_shape=(jax.ShapeDtypeStruct((8, 3 * D)...  3.02 us
  transfers between devices with their start and end apart: 1, of which 1 were waited for; matrix products, arithmetic and copies ran while one was open for 0% of the time, Pallas kernels for 5%

profile of v6, /device:TPU:1, one launch (start us, length us, event | category | flops | bytes accessed | tf_op | source)
XLA Modules:
  0.0 58.4 jit_solution(9948624740449549156)
XLA Ops:
  1.3 0.0 copy-start.2
  1.3 8.8 %spatial.1 = bf16[128,2,1152]{2,1,0:T(2,128)(2,1)} custom-call(s32[1]{0:T(128)S(6)} %copy.14.step_ref, bf16[256,1152]{1,0:T(8,128)(2,1)} %hidden_hbm.1, bf16[256,6912]{1,0:T(8,128)(2,1)} %time_hbm.3, bf16[1152,3456]{1,0:T(8,128)(2,1)} %qkv_hbm.4, bf16[1152,1152]{1,0:T(8,128)(2,1)} %out_hbm.2), custom_call_target="tpu_custom_call" | custom-call | flops 4294967296 | bytes 14680064 | tf_op jit(solution)/shard_map/spatial/pallas_call | solution.py:317
  10.1 11.5 %all-to-all-start = ((bf16[128,2,1152]{2,1,0:T(2,128)(2,1)}), bf16[128,2,1152]{2,1,0:T(2,128)(2,1)S(1)}, u32[]{:S(2)}, u32[]{:S(2)}) async-start(bf16[128,2,1152]{2,1,0:T(2,128)(2,1)} %spatial.1), calls=%async_computation | async-start | bytes 1179648 | tf_op jit(solution)/shard_map/all_to_all | solution.py:340
  22.3 0.0 copy-done.2
  22.3 3.0 %prepare.1 = (f32[8,3456]{1,0:T(8,128)S(1)}, bf16[1152,1024]{1,0:T(8,128)(2,1)S(1)}, f32[32,128]{1,0:T(8,128)S(1)}, bf16[1152,128]{1,0:T(8,128)(2,1)S(1)}) custom-call(s32[1]{0:T(128)S(6)} %copy.14.step_ref, s32[1]{0:T(128)S(6)} %copy.15.tag_ref, f32[8]{0:T(128)S(1)} %copy-done.2, bf16[256,6912]{1,0:T(8,128)(2,1)} %time_hbm.3, bf16[1152,3456]{1,0:T(8,128)(2,1)} %qkv_hbm.5, ...), custom_call_target="tpu_custom_call" | custom-call | flops 33554432 | bytes 8388608 | tf_op jit(solution)/shard_map/prepare/pallas_call | solution.py:343
  25.3 10.4 %all-to-all-done.arrived_ref = bf16[128,2,1152]{2,1,0:T(2,128)(2,1)S(1)} async-done(((bf16[128,2,1152]{2,1,0:T(2,128)(2,1)}), bf16[128,2,1152]{2,1,0:T(2,128)(2,1)S(1)}, u32[]{:S(2)}, u32[]{:S(2)}) %all-to-all-start) | async-done | bytes 589856 | tf_op jit(solution)/shard_map/all_to_all | solution.py:340
  35.8 0.0 copy-start
  35.8 0.0 copy-start.1
  35.8 7.3 %temporal.1 = f32[256,128]{1,0:T(8,128)S(1)} custom-call(bf16[128,2,1152]{2,1,0:T(2,128)(2,1)S(1)} %all-to-all-done.arrived_ref, f32[8,3456]{1,0:T(8,128)S(1)} %get-tuple-element.7.table, bf16[1152,1024]{1,0:T(8,128)(2,1)S(1)} %get-tuple-element.8.early, bf16[1152,128]{1,0:T(8,128)(2,1)S(1)} %get-tuple-element.9.head_weight, bf16[1152,3456]{1,0:T(8,128)(2,1)} %qkv_hbm.5, ...), custom_call_target="tpu_custom_call" | custom-call | flops 4294967296 | bytes 12582912 | tf_op jit(solution)/shard_map/temporal/pallas_call | solution.py:367
  43.1 14.6 %all_to_all.10 = f32[128,2,128]{2,1,0:T(2,128)S(1)} all-to-all(f32[128,2,128]{2,1,0:T(2,128)S(1)} %bitcast.3), channel_id=1, replica_groups=mesh['inner'=32,'outer'=4] {'inner','outer'}, dimensions={0} | all-to-all | bytes 262144 | tf_op jit(solution)/shard_map/all_to_all | solution.py:389
  57.7 0.0 copy-done
  57.7 0.0 copy-done.1
  57.7 0.7 %density.1 = (f32[1,256]{1,0:T(1,128)}, f32[1,16,256]{2,1,0:T(8,128)}) custom-call(f32[32,128]{1,0:T(8,128)S(1)} %get-tuple-element.6.terms_ref, f32[256,128]{1,0:T(8,128)S(1)} %bitcast.2, f32[1,16,256]{2,1,0:T(8,128)S(1)} %copy-done, f32[1,16,256]{2,1,0:T(8,128)S(1)} %copy-done.1), custom_call_target="tpu_custom_call" | custom-call | tf_op jit(solution)/shard_map/density/pallas_call | solution.py:396
Async XLA Ops:
  1.3 21.0 %copy-start.2 = (f32[8]{0:T(128)S(1)}, f32[8]{0:T(128)}, u32[]{:S(2)}) copy-start(f32[8]{0:T(128)} %level_ref.1) | copy-start | bytes 100
  10.1 25.6 %all-to-all-start = ((bf16[128,2,1152]{2,1,0:T(2,128)(2,1)}), bf16[128,2,1152]{2,1,0:T(2,128)(2,1)S(1)}, u32[]{:S(2)}, u32[]{:S(2)}) async-start(bf16[128,2,1152]{2,1,0:T(2,128)(2,1)} %spatial.1), calls=%async_computation | async-start | bytes 1179648 | tf_op jit(solution)/shard_map/all_to_all | solution.py:340
  35.8 22.0 %copy-start = (f32[1,16,256]{2,1,0:T(8,128)S(1)}, f32[1,16,256]{2,1,0:T(8,128)}, u32[]{:S(2)}) copy-start(f32[1,16,256]{2,1,0:T(8,128)} %now_ref.1) | copy-start | bytes 49156
  35.8 22.0 %copy-start.1 = (f32[1,16,256]{2,1,0:T(8,128)S(1)}, f32[1,16,256]{2,1,0:T(8,128)}, u32[]{:S(2)}) copy-start(f32[1,16,256]{2,1,0:T(8,128)} %next_ref.1) | copy-start | bytes 49156

commit v7 on v6

--- a/solution.py
+++ b/solution.py
@@ -17,7 +17,7 @@
 TPF = 256
 LANES = 128
 OUT_CHUNKS = tuple((low, min(512, D - low)) for low in range(0, D, 512))
-CUTS = (0, 512, 1280, 2 * D, 3 * D)
+CUTS = (0, 256, 1024, 2 * D, 3 * D)
 EARLY = 1024
 ROWS = 32
 

time: 58.7 us -> 58.6 us (level)
  no operation moved by 1% of the time
where the time goes in v7:
time: 58.6 us; the launch traced here: 58.4 us
  Pallas kernels  19.9 us (34%)
  blocking collectives  14.6 us (25%)
  starting transfers between devices  11.5 us (20%)
  waiting for transfers between devices  10.4 us (18%)
  between operations  1.97 us (3%)
    all_to_all x1, blocking collectives, shards(): lax.all_to_all(velocity.reshape(TPF // 2, 2, LANES), ('inner', 'outer'),...  14.6 us
    all_to_all x1, starting transfers between devices, shards(): lax.all_to_all(after_spatial, ('inner', 'outer'), split_axis=0, concat_ax...  11.5 us
    all_to_all x1, waiting for transfers between devices, shards(): lax.all_to_all(after_spatial, ('inner', 'outer'), split_axis=0, concat_ax...  10.4 us
    pallas_call x1, Pallas kernels, shards(): pl.pallas_call(spatial_kernel, out_shape=jax.ShapeDtypeStruct((TPF // 2,...  8.8 us
    pallas_call x1, Pallas kernels, shards(): pl.pallas_call(temporal_kernel, out_shape=jax.ShapeDtypeStruct((TPF, LANE...  7.34 us
    pallas_call x1, Pallas kernels, shards(): pl.pallas_call(prepare_kernel, out_shape=(jax.ShapeDtypeStruct((8, 3 * D)...  3.02 us
  transfers between devices with their start and end apart: 1, of which 1 were waited for; matrix products, arithmetic and copies ran while one was open for 0% of the time, Pallas kernels for 5%

profile of v7, /device:TPU:1, one launch (start us, length us, event | category | flops | bytes accessed | tf_op | source)
XLA Modules:
  0.0 58.4 jit_solution(5685872718658650672)
XLA Ops:
  1.3 0.0 copy-start.2
  1.3 8.8 %spatial.1 = bf16[128,2,1152]{2,1,0:T(2,128)(2,1)} custom-call(s32[1]{0:T(128)S(6)} %copy.14.step_ref, bf16[256,1152]{1,0:T(8,128)(2,1)} %hidden_hbm.1, bf16[256,6912]{1,0:T(8,128)(2,1)} %time_hbm.3, bf16[1152,3456]{1,0:T(8,128)(2,1)} %qkv_hbm.4, bf16[1152,1152]{1,0:T(8,128)(2,1)} %out_hbm.2), custom_call_target="tpu_custom_call" | custom-call | flops 4294967296 | bytes 14680064 | tf_op jit(solution)/shard_map/spatial/pallas_call | solution.py:317
  10.1 11.5 %all-to-all-start = ((bf16[128,2,1152]{2,1,0:T(2,128)(2,1)}), bf16[128,2,1152]{2,1,0:T(2,128)(2,1)S(1)}, u32[]{:S(2)}, u32[]{:S(2)}) async-start(bf16[128,2,1152]{2,1,0:T(2,128)(2,1)} %spatial.1), calls=%async_computation | async-start | bytes 1179648 | tf_op jit(solution)/shard_map/all_to_all | solution.py:340
  22.3 0.0 copy-done.2
  22.3 3.0 %prepare.1 = (f32[8,3456]{1,0:T(8,128)S(1)}, bf16[1152,1024]{1,0:T(8,128)(2,1)S(1)}, f32[32,128]{1,0:T(8,128)S(1)}, bf16[1152,128]{1,0:T(8,128)(2,1)S(1)}) custom-call(s32[1]{0:T(128)S(6)} %copy.14.step_ref, s32[1]{0:T(128)S(6)} %copy.15.tag_ref, f32[8]{0:T(128)S(1)} %copy-done.2, bf16[256,6912]{1,0:T(8,128)(2,1)} %time_hbm.3, bf16[1152,3456]{1,0:T(8,128)(2,1)} %qkv_hbm.5, ...), custom_call_target="tpu_custom_call" | custom-call | flops 33554432 | bytes 8388608 | tf_op jit(solution)/shard_map/prepare/pallas_call | solution.py:343
  25.3 10.4 %all-to-all-done.arrived_ref = bf16[128,2,1152]{2,1,0:T(2,128)(2,1)S(1)} async-done(((bf16[128,2,1152]{2,1,0:T(2,128)(2,1)}), bf16[128,2,1152]{2,1,0:T(2,128)(2,1)S(1)}, u32[]{:S(2)}, u32[]{:S(2)}) %all-to-all-start) | async-done | bytes 589856 | tf_op jit(solution)/shard_map/all_to_all | solution.py:340
  35.7 0.0 copy-start
  35.7 0.0 copy-start.1
  35.7 7.3 %temporal.1 = f32[256,128]{1,0:T(8,128)S(1)} custom-call(bf16[128,2,1152]{2,1,0:T(2,128)(2,1)S(1)} %all-to-all-done.arrived_ref, f32[8,3456]{1,0:T(8,128)S(1)} %get-tuple-element.7.table, bf16[1152,1024]{1,0:T(8,128)(2,1)S(1)} %get-tuple-element.8.early, bf16[1152,128]{1,0:T(8,128)(2,1)S(1)} %get-tuple-element.9.head_weight, bf16[1152,3456]{1,0:T(8,128)(2,1)} %qkv_hbm.5, ...), custom_call_target="tpu_custom_call" | custom-call | flops 4294967296 | bytes 12582912 | tf_op jit(solution)/shard_map/temporal/pallas_call | solution.py:367
  43.1 14.6 %all_to_all.10 = f32[128,2,128]{2,1,0:T(2,128)S(1)} all-to-all(f32[128,2,128]{2,1,0:T(2,128)S(1)} %bitcast.3), channel_id=1, replica_groups=mesh['inner'=32,'outer'=4] {'inner','outer'}, dimensions={0} | all-to-all | bytes 262144 | tf_op jit(solution)/shard_map/all_to_all | solution.py:389
  57.7 0.0 copy-done
  57.7 0.0 copy-done.1
  57.7 0.7 %density.1 = (f32[1,256]{1,0:T(1,128)}, f32[1,16,256]{2,1,0:T(8,128)}) custom-call(f32[32,128]{1,0:T(8,128)S(1)} %get-tuple-element.6.terms_ref, f32[256,128]{1,0:T(8,128)S(1)} %bitcast.2, f32[1,16,256]{2,1,0:T(8,128)S(1)} %copy-done, f32[1,16,256]{2,1,0:T(8,128)S(1)} %copy-done.1), custom_call_target="tpu_custom_call" | custom-call | tf_op jit(solution)/shard_map/density/pallas_call | solution.py:396
Async XLA Ops:
  1.3 21.0 %copy-start.2 = (f32[8]{0:T(128)S(1)}, f32[8]{0:T(128)}, u32[]{:S(2)}) copy-start(f32[8]{0:T(128)} %level_ref.1) | copy-start | bytes 100
  10.1 25.6 %all-to-all-start = ((bf16[128,2,1152]{2,1,0:T(2,128)(2,1)}), bf16[128,2,1152]{2,1,0:T(2,128)(2,1)S(1)}, u32[]{:S(2)}, u32[]{:S(2)}) async-start(bf16[128,2,1152]{2,1,0:T(2,128)(2,1)} %spatial.1), calls=%async_computation | async-start | bytes 1179648 | tf_op jit(solution)/shard_map/all_to_all | solution.py:340
  35.7 22.0 %copy-start = (f32[1,16,256]{2,1,0:T(8,128)S(1)}, f32[1,16,256]{2,1,0:T(8,128)}, u32[]{:S(2)}) copy-start(f32[1,16,256]{2,1,0:T(8,128)} %now_ref.1) | copy-start | bytes 49156
  35.7 22.0 %copy-start.1 = (f32[1,16,256]{2,1,0:T(8,128)S(1)}, f32[1,16,256]{2,1,0:T(8,128)}, u32[]{:S(2)}) copy-start(f32[1,16,256]{2,1,0:T(8,128)} %next_ref.1) | copy-start | bytes 49156
